TPU v7x, 512 devices: a whole 4x4x16 slice. The times are simulated.
512 devices in a mesh: ctx: 32 (over x, y, core), head: 16 (over z).
Axes of the slice: x: 4, y: 4, z: 16, core: 2. Of those that a mesh axis runs over, the one named last changes fastest.
Arguments:
- mixed_in: bfloat16 [8192, 8192], P(('ctx', 'head')), may hold values from -6 to 6
- conv_weight: float32 [4, 8192], P(None, 'head'), may hold values from -3 to 3
- write_strength_logit: float32 [32, 8192], P('head', 'ctx'), may hold values from -10.5 to 2.2, as said below
- decay_log: float32 [32, 8192], P('head', 'ctx'), may hold values from -0.7 to 0, as said below
- initial_state: float32 [32, 128, 128], P('head'), may hold values from -6 to 6
- final_state_grad: float32 [32, 128, 128], P('head'), may hold values from -6 to 6
- grad_out: bfloat16 [8192, 4096], P('ctx', 'head'), may hold values from -6 to 6
Outputs:
- grad_mixed: bfloat16 [8192, 8192], P(('ctx', 'head'))
- grad_conv: float32 [4, 8192], P(None, 'head')
- grad_beta_logit: float32 [32, 8192], P('head', 'ctx')
- grad_decay_log: float32 [32, 8192], P('head', 'ctx')
Inputs may be any that keep to these rules, and one draw needn't show every extreme that they name: `write_strength_logit`: each value head's write strengths and decays vary from token to token. `decay_log`: every entry is negative.
All inputs are finite; a program needn't handle non-finite values.
Results may differ from a plain program's by a relative error of at most 0.001.
Values may be sent and summed in bfloat16 or wider, within the bound.
A program may use at most 64 MiB of HBM per device.

v0:
```python
import jax
import jax.numpy as jnp
from jax import lax
from jax.sharding import PartitionSpec as P

HK = 16
VALUE_HEADS = 32
DK = 128
DV = 128
KW = 4
BLOCK = 64


highest = lax.Precision.HIGHEST
norm_eps = 1e-06


def from_behind(value, axis, by):
    devices = lax.axis_size(axis)
    pairs = [(i, i + by) for i in range(devices) if 0 <= i + by < devices]
    return lax.ppermute(value, axis, pairs)


def prefix(value, axis, combine, identity, reverse):
    devices, mine = (lax.axis_size(axis), lax.axis_index(axis))
    everything = jax.tree.map(lambda part: lax.all_gather(part, axis), value)
    start = jax.tree.map(
        lambda part, zero: jnp.broadcast_to(jnp.asarray(zero, part.dtype), part.shape),
        value,
        identity,
    )

    def step(k, before):
        at = devices - 1 - k if reverse else k
        reached = at > mine if reverse else at < mine
        new = combine(before, jax.tree.map(lambda part: part[at], everything))
        return jax.tree.map(lambda a, b: jnp.where(reached, a, b), new, before)

    return lax.fori_loop(0, devices, step, start)


def block_step(carried, pieces):
    state, transit = carried
    queries, key_feats, values, beta_gate, log_decay = pieces
    block_size = log_decay.shape[0]
    cumulative = jnp.cumsum(log_decay)
    row_ids = lax.broadcasted_iota(jnp.int32, (block_size, block_size), 0)
    col_ids = lax.broadcasted_iota(jnp.int32, (block_size, block_size), 1)
    causal = col_ids <= row_ids
    differ = jnp.where(causal, cumulative[:, None] - cumulative[None, :], 0.0)
    ratios = jnp.where(causal, jnp.exp(differ), 0.0)
    key_gram = jnp.dot(key_feats, key_feats.T, precision=highest)
    lower_part = jnp.where(col_ids < row_ids, beta_gate[:, None] * ratios * key_gram, 0.0)
    system = lower_part + jnp.eye(block_size, dtype=jnp.float32)
    decays = jnp.exp(cumulative)
    right_sides = jnp.concatenate(
        [beta_gate[:, None] * values, (beta_gate * decays)[:, None] * key_feats], axis=1
    )
    solved = jax.scipy.linalg.solve_triangular(system, right_sides, lower=True)
    width_v = values.shape[1]
    base_update = solved[:, :width_v]
    weights = solved[:, width_v:]
    update = base_update - jnp.dot(weights, state, precision=highest)
    scores = ratios * jnp.dot(queries, key_feats.T, precision=highest)
    output = decays[:, None] * jnp.dot(queries, state, precision=highest) + jnp.dot(
        scores, update, precision=highest
    )
    total_decay = jnp.exp(cumulative[-1])
    tail_keys = jnp.exp(cumulative[-1] - cumulative)[:, None] * key_feats
    new_state = total_decay * state + jnp.dot(tail_keys.T, update, precision=highest)
    step_map = total_decay * jnp.eye(key_feats.shape[1], dtype=jnp.float32) - jnp.dot(
        tail_keys.T, weights, precision=highest
    )
    new_transit = jnp.dot(step_map, transit, precision=highest)
    return ((new_state, new_transit), output)


def run_head(state, queries, key_feats, values, beta_gate, log_decay):
    blocks = queries.shape[0] // BLOCK
    pieces = (
        queries.reshape(blocks, BLOCK, -1),
        key_feats.reshape(blocks, BLOCK, -1),
        values.reshape(blocks, BLOCK, -1),
        beta_gate.reshape(blocks, BLOCK),
        log_decay.reshape(blocks, BLOCK),
    )
    start = (state, jnp.eye(key_feats.shape[1], dtype=jnp.float32))
    (state_end, transit), outputs = lax.scan(block_step, start, pieces)
    return (outputs.reshape(-1, values.shape[1]), state_end, transit)


def normalize(feats, factor):
    return feats * lax.rsqrt(jnp.sum(feats * feats, axis=-1, keepdims=True) + norm_eps) * factor


def mix_layer(state_in, extended, conv_weight, write_strength_logit, decay_log):
    row_count = extended.shape[0] - (KW - 1)
    filtered_signal = conv_weight[0] * extended[0:row_count]
    for tap in range(1, KW):
        filtered_signal = filtered_signal + conv_weight[tap] * extended[tap : tap + row_count]
    activated = jax.nn.silu(filtered_signal)
    ratio_heads = VALUE_HEADS // HK
    group_width = 2 * DK + ratio_heads * DV
    groups = activated.reshape(row_count, -1, group_width)
    key_heads = groups.shape[1]
    queries = normalize(groups[:, :, :DK], DK ** (-0.5))
    key_feats = normalize(groups[:, :, DK : 2 * DK], 1.0)
    values = (
        groups[:, :, 2 * DK :].reshape(row_count, key_heads * ratio_heads, DV).transpose(1, 0, 2)
    )
    queries = jnp.repeat(queries.transpose(1, 0, 2), ratio_heads, axis=0)
    key_feats = jnp.repeat(key_feats.transpose(1, 0, 2), ratio_heads, axis=0)
    beta_gate = jax.nn.sigmoid(write_strength_logit)
    outputs, state_out, transit = jax.vmap(run_head)(
        state_in, queries, key_feats, values, beta_gate, decay_log
    )
    result = outputs.transpose(1, 0, 2).reshape(row_count, -1)
    return ((result, state_out), transit)


def compose(earlier, later):
    matrix = jnp.einsum("hij,hjk->hik", later[0], earlier[0], precision=highest)
    offset = jnp.einsum("hij,hjk->hik", later[0], earlier[1], precision=highest) + later[1]
    return (matrix, offset)


def advance(maps, state):
    return jnp.einsum("hij,hjk->hik", maps[0], state, precision=highest) + maps[1]


def on_device(
    mixed_in,
    conv_weight,
    write_strength_logit,
    decay_log,
    initial_state,
    final_state_grad,
    grad_out,
):
    local_in = lax.all_to_all(mixed_in, "head", split_axis=1, concat_axis=0, tiled=True)
    edge_rows = from_behind(local_in[-(KW - 1) :], "ctx", 1)
    extended = jnp.concatenate([edge_rows, local_in], axis=0).astype(jnp.float32)
    cotangent = grad_out.astype(jnp.float32)
    zeros_state = jnp.zeros_like(initial_state)

    def from_state(state):
        return mix_layer(state, extended, conv_weight, write_strength_logit, decay_log)

    primal, pull_state, transit = jax.vjp(from_state, zeros_state, has_aux=True)
    offset = primal[1]
    local_grad = pull_state((cotangent, jnp.zeros_like(offset)))[0]
    flipped = jnp.swapaxes(transit, 1, 2)
    identity = (
        jnp.broadcast_to(jnp.eye(transit.shape[1], dtype=jnp.float32), transit.shape),
        jnp.zeros_like(offset),
    )
    earlier_map = prefix((transit, offset), "ctx", compose, identity, False)
    later_map = prefix((flipped, local_grad), "ctx", compose, identity, True)
    state_in = advance(earlier_map, initial_state)
    state_grad = advance(later_map, final_state_grad)

    def forward(ext_rows, weight_taps, logits, decay_logs):
        return mix_layer(state_in, ext_rows, weight_taps, logits, decay_logs)

    unused, pull_all, unused_transit = jax.vjp(
        forward, extended, conv_weight, write_strength_logit, decay_log, has_aux=True
    )
    grad_ext, grad_weight, grad_beta, grad_decay = pull_all((cotangent, state_grad))
    spilled = from_behind(grad_ext[: KW - 1], "ctx", -1)
    own_grad = grad_ext[KW - 1 :]
    own_grad = jnp.concatenate([own_grad[: -(KW - 1)], own_grad[-(KW - 1) :] + spilled], axis=0)
    returned = lax.all_to_all(
        own_grad.astype(jnp.bfloat16), "head", split_axis=0, concat_axis=1, tiled=True
    )
    weight_total = lax.psum(grad_weight, "ctx")
    return (returned, weight_total, grad_beta, grad_decay)


def solution(mesh):
    in_specs = (
        P(("ctx", "head"), None),
        P(None, "head"),
        P("head", "ctx"),
        P("head", "ctx"),
        P("head", None, None),
        P("head", None, None),
        P("ctx", "head"),
    )
    out_specs = (P(("ctx", "head"), None), P(None, "head"), P("head", "ctx"), P("head", "ctx"))
    return jax.shard_map(
        on_device, mesh=mesh, in_specs=in_specs, out_specs=out_specs, check_vma=False
    )
```

profile of v0, /device:TPU:1, one launch (start us, length us, event | category | flops | bytes accessed | tf_op | source)
XLA Modules:
  0.0 794.1 jit_solution(5155768118002871086)
XLA Ops:
  8.9 15.7 %all-to-all-start = ((bf16[16,16,512]{2,0,1:T(8,128)(2,1)}), bf16[16,16,512]{2,0,1:T(8,128)(2,1)S(1)}, u32[]{:S(2)}, u32[]{:S(2)}) async-start(bf16[16,16,512]{2,0,1:T(8,128)(2,1)} %bitcast.435), calls=%async_computation | async-start | bytes 524288 | tf_op jit(solution)/shard_map/all_to_all | solution.py:140
  26.9 10.9 %all-to-all-done = bf16[16,16,512]{2,0,1:T(8,128)(2,1)S(1)} async-done(((bf16[16,16,512]{2,0,1:T(8,128)(2,1)}), bf16[16,16,512]{2,0,1:T(8,128)(2,1)S(1)}, u32[]{:S(2)}, u32[]{:S(2)}) %all-to-all-start) | async-done | bytes 262176 | tf_op jit(solution)/shard_map/all_to_all | solution.py:140
  37.8 9.3 %collective-permute-start = (bf16[3,512]{1,0:T(4,128)(2,1)S(1)}, bf16[3,512]{1,0:T(4,128)(2,1)S(1)}, u32[]{:S(2)}, u32[]{:S(2)}) collective-permute-start(bf16[3,512]{1,0:T(4,128)(2,1)S(1)} %slice.149), channel_id=1, source_target_pairs={{0,16},{16,32},{32,48},{48,64},{64,80},{80,96},{96,112},{112,128},... | collective-permute-start | bytes 9224 | tf_op jit(solution)/shard_map/ppermute | solution.py:21
  52.3 65.6 %while.169 = (s32[]{:T(128)}, f32[2,128,128]{2,1,0:T(8,128)S(1)}, f32[2,128,128]{2,1,0:T(8,128)S(1)}, f32[4,2,64,128]{3,2,1,0:T(8,128)S(1)}, f32[4,2,64,1]{2,1,3...) while((s32[]{:T(128)}, f32[2,128,128]{2,1,0:T(8,128)S(1)}, ...), condition=%wide.region_4.6_spmd.clone.clone, body=%wide.region_2.5_spmd.clone.clone.sunk | while | flops 176640128 | bytes 2980628 | solution.py:88
  55.3 9.8 %custom-call.35 = f32[2,1,64,64]{2,3,1,0:T(8,128)S(1)} custom-call(f32[2,1,64,64]{3,2,1,0:T(8,128)S(1)} %fusion.420), custom_call_target="InvertDiagBlocksLowerTriangular" | custom-call | tf_op jit(solution)/shard_map/jvp(vmap())/while/body/eval_jaxpr/jit(_solve_triangular)/triangular_solve/custom-call.1 | solution.py:59
  71.6 9.8 %custom-call.35 = f32[2,1,64,64]{2,3,1,0:T(8,128)S(1)} custom-call(f32[2,1,64,64]{3,2,1,0:T(8,128)S(1)} %fusion.420), custom_call_target="InvertDiagBlocksLowerTriangular" | custom-call | tf_op jit(solution)/shard_map/jvp(vmap())/while/body/eval_jaxpr/jit(_solve_triangular)/triangular_solve/custom-call.1 | solution.py:59
  88.0 9.8 %custom-call.35 = f32[2,1,64,64]{2,3,1,0:T(8,128)S(1)} custom-call(f32[2,1,64,64]{3,2,1,0:T(8,128)S(1)} %fusion.420), custom_call_target="InvertDiagBlocksLowerTriangular" | custom-call | tf_op jit(solution)/shard_map/jvp(vmap())/while/body/eval_jaxpr/jit(_solve_triangular)/triangular_solve/custom-call.1 | solution.py:59
  104.4 9.8 %custom-call.35 = f32[2,1,64,64]{2,3,1,0:T(8,128)S(1)} custom-call(f32[2,1,64,64]{3,2,1,0:T(8,128)S(1)} %fusion.420), custom_call_target="InvertDiagBlocksLowerTriangular" | custom-call | tf_op jit(solution)/shard_map/jvp(vmap())/while/body/eval_jaxpr/jit(_solve_triangular)/triangular_solve/custom-call.1 | solution.py:59
  120.7 9.2 %while.166 = (s32[]{:T(128)}, f32[2,128,128]{2,1,0:T(8,128)S(1)}, f32[4,2,1,1]{1,3,2,0:T(1,128)S(1)}, f32[4,2,64,128]{3,2,1,0:T(8,128)S(1)}, f32[4,2,64,1]{2,1,3...) while((s32[]{:T(128)}, f32[2,128,128]{2,1,0:T(8,128)S(1)}, ...), condition=%wide.region_6.8_spmd.clone, body=%wide.region_5.7_spmd.clone.sunk | while | flops 88293376 | bytes 1316019 | solution.py:88
  131.9 42.9 %all-gather.9.cloned.1.call-done = f32[64,128,128]{2,1,0:T(8,128)} async-done(((f32[2,128,128]{2,1,0:T(8,128)}), f32[64,128,128]{2,1,0:T(8,128)}) %all-gather.9.cloned.1.call-update) | async-done | bytes 4194320 | tf_op jit(solution)/shard_map/all_gather | solution.py:26
  174.8 64.6 %all-gather.11.cloned.1.call-done = f32[64,128,128]{2,1,0:T(8,128)} async-done(((f32[2,128,128]{2,1,0:T(8,128)}), f32[64,128,128]{2,1,0:T(8,128)}) %all-gather.11.cloned.1.call-update) | async-done | bytes 4194320 | tf_op jit(solution)/shard_map/all_gather | solution.py:26
  239.5 80.1 %while.167 = (s32[]{:T(128)}, f32[2,128,128]{2,1,0:T(8,128)S(1)}, f32[2,128,128]{2,1,0:T(8,128)S(1)}, s32[]{:T(128)}, f32[32,2,128,128]{3,2,1,0:T(8,128)}, /*ind...) while((s32[]{:T(128)}, f32[2,128,128]{2,1,0:T(8,128)S(1)}, ...), condition=%wide.region_8.10_spmd.clone, body=%wide.region_7.9_spmd.clone.sunk | while | flops 100827144 | bytes 1706674 | solution.py:39
  319.6 47.8 %all-gather.15.cloned.1.call-done = f32[64,128,128]{2,1,0:T(8,128)} async-done(((f32[2,128,128]{2,1,0:T(8,128)}), f32[64,128,128]{2,1,0:T(8,128)}) %all-gather.15.cloned.1.call-update) | async-done | bytes 4194320 | tf_op jit(solution)/shard_map/all_gather | solution.py:26
  367.5 79.6 %while.168 = (s32[]{:T(128)}, f32[2,128,128]{2,1,0:T(8,128)S(1)}, f32[2,128,128]{2,1,0:T(8,128)S(1)}, s32[]{:T(128)}, f32[32,2,128,128]{3,2,1,0:T(8,128)}, /*ind...) while((s32[]{:T(128)}, f32[2,128,128]{2,1,0:T(8,128)S(1)}, f32[2,128,128]{2,1,0:T(8,128)S(1)}, ...), condition=%wide.region_10.12_spmd.clone, body=%wide.region_9.11_spmd.clone.sunk | while | flops 100827136 | bytes 1706612 | solution.py:39
  459.6 107.3 %while.164 = (s32[]{:T(128)}, f32[2,128,128]{2,1,0:T(8,128)S(1)}, f32[4,2,64,64]{3,2,1,0:T(8,128)}, f32[4,2,128,64]{2,3,1,0:T(8,128)}, f32[4,2,64,64]{3,2,1,0:T(...) while((s32[]{:T(128)}, f32[2,128,128]{2,1,0:T(8,128)S(1)}, ...), condition=%wide.region_13.15_spmd.clone.clone, body=%wide.region_11.14_spmd.clone.clone.sunk | while | flops 126194176 | bytes 3312057 | solution.py:88
  464.6 11.2 %custom-call.33 = f32[2,1,64,64]{2,3,1,0:T(8,128)} custom-call(f32[2,1,64,64]{3,2,1,0:T(8,128)} %select_bitcast_fusion.4), custom_call_target="InvertDiagBlocksLowerTriangular" | custom-call | tf_op jit(solution)/shard_map/jvp(vmap())/while/body/eval_jaxpr/jit(_solve_triangular)/triangular_solve/custom-call.1 | solution.py:59
  475.8 1.8 bitcast_dynamic-update-slice_fusion.22
  491.4 11.2 %custom-call.33 = f32[2,1,64,64]{2,3,1,0:T(8,128)} custom-call(f32[2,1,64,64]{3,2,1,0:T(8,128)} %select_bitcast_fusion.4), custom_call_target="InvertDiagBlocksLowerTriangular" | custom-call | tf_op jit(solution)/shard_map/jvp(vmap())/while/body/eval_jaxpr/jit(_solve_triangular)/triangular_solve/custom-call.1 | solution.py:59
  502.6 1.8 bitcast_dynamic-update-slice_fusion.22
  518.3 11.2 %custom-call.33 = f32[2,1,64,64]{2,3,1,0:T(8,128)} custom-call(f32[2,1,64,64]{3,2,1,0:T(8,128)} %select_bitcast_fusion.4), custom_call_target="InvertDiagBlocksLowerTriangular" | custom-call | tf_op jit(solution)/shard_map/jvp(vmap())/while/body/eval_jaxpr/jit(_solve_triangular)/triangular_solve/custom-call.1 | solution.py:59
  529.4 1.8 bitcast_dynamic-update-slice_fusion.22
  545.1 11.2 %custom-call.33 = f32[2,1,64,64]{2,3,1,0:T(8,128)} custom-call(f32[2,1,64,64]{3,2,1,0:T(8,128)} %select_bitcast_fusion.4), custom_call_target="InvertDiagBlocksLowerTriangular" | custom-call | tf_op jit(solution)/shard_map/jvp(vmap())/while/body/eval_jaxpr/jit(_solve_triangular)/triangular_solve/custom-call.1 | solution.py:59
  556.3 1.8 bitcast_dynamic-update-slice_fusion.22
  570.9 127.3 %while.165 = (s32[]{:T(128)}, f32[2,128,128]{2,1,0:T(8,128)S(1)}, f32[4,2,64,128]{3,2,1,0:T(8,128)}, f32[4,2,64,128]{3,2,1,0:T(8,128)}, f32[4,2,64,128]{3,2,0,1:...) while((s32[]{:T(128)}, f32[2,128,128]{2,1,0:T(8,128)S(1)}, ...), condition=%wide.region_25.27_spmd.clone.clone, body=%wide.region_14.26_spmd.clone.clone.sunk | while | flops 283857920 | bytes 5617773 | solution.py:88
  574.5 9.8 %custom-call.34 = f32[2,1,64,64]{2,3,1,0:T(8,128)S(1)} custom-call(f32[2,1,64,64]{3,2,1,0:T(8,128)S(1)} %select_bitcast_fusion.5), custom_call_target="InvertDiagBlocksLowerTriangular" | custom-call | tf_op jit(solution)/shard_map/transpose(jvp(vmap()))/while/body/eval_jaxpr/jit(_solve_triangular)/triangular_solve | solution.py:59
  606.4 9.8 %custom-call.34 = f32[2,1,64,64]{2,3,1,0:T(8,128)S(1)} custom-call(f32[2,1,64,64]{3,2,1,0:T(8,128)S(1)} %select_bitcast_fusion.5), custom_call_target="InvertDiagBlocksLowerTriangular" | custom-call | tf_op jit(solution)/shard_map/transpose(jvp(vmap()))/while/body/eval_jaxpr/jit(_solve_triangular)/triangular_solve | solution.py:59
  638.2 9.8 %custom-call.34 = f32[2,1,64,64]{2,3,1,0:T(8,128)S(1)} custom-call(f32[2,1,64,64]{3,2,1,0:T(8,128)S(1)} %select_bitcast_fusion.5), custom_call_target="InvertDiagBlocksLowerTriangular" | custom-call | tf_op jit(solution)/shard_map/transpose(jvp(vmap()))/while/body/eval_jaxpr/jit(_solve_triangular)/triangular_solve | solution.py:59
  670.0 9.8 %custom-call.34 = f32[2,1,64,64]{2,3,1,0:T(8,128)S(1)} custom-call(f32[2,1,64,64]{3,2,1,0:T(8,128)S(1)} %select_bitcast_fusion.5), custom_call_target="InvertDiagBlocksLowerTriangular" | custom-call | tf_op jit(solution)/shard_map/transpose(jvp(vmap()))/while/body/eval_jaxpr/jit(_solve_triangular)/triangular_solve | solution.py:59
  705.2 2.2 collective-permute-start.1
  707.7 2.4 collective-permute-done.1
  710.9 12.0 %all-to-all-start.1 = ((bf16[16,16,512]{2,1,0:T(8,128)(2,1)}), bf16[16,16,512]{2,1,0:T(8,128)(2,1)S(1)}, u32[]{:S(2)}, u32[]{:S(2)}) async-start(bf16[16,16,512]{2,1,0:T(8,128)(2,1)} %bitcast.32), calls=%async_computation.1 | async-start | bytes 524288 | tf_op jit(solution)/shard_map/all_to_all | solution.py:172
  723.7 62.5 %psum.7 = f32[4,512]{1,0:T(4,128)} all-reduce(f32[4,512]{1,0:T(4,128)S(1)} %pad_add_fusion.5), channel_id=1, replica_groups=mesh['ctx'=32,'head'=16] {'ctx'}, use_global_device_ids=true, to_apply=%region_34.36 | all-reduce | flops 2048 | bytes 16384 | tf_op jit(solution)/shard_map/psum | solution.py:175
  (740 shorter events, 373.4 us)
Async XLA Ops:
  7.2 440.0 %copy-start = (f32[2,128,128]{2,1,0:T(8,128)S(1)}, f32[2,128,128]{2,1,0:T(8,128)}, u32[]{:S(2)}) copy-start(f32[2,128,128]{2,1,0:T(8,128)} %param.25) | copy-start | bytes 393220
  8.9 28.9 %all-to-all-start = ((bf16[16,16,512]{2,0,1:T(8,128)(2,1)}), bf16[16,16,512]{2,0,1:T(8,128)(2,1)S(1)}, u32[]{:S(2)}, u32[]{:S(2)}) async-start(bf16[16,16,512]{2,0,1:T(8,128)(2,1)} %bitcast.435), calls=%async_computation | async-start | bytes 524288 | tf_op jit(solution)/shard_map/all_to_all | solution.py:140
  24.6 150.2 %all-gather.9.cloned.1.call-start = ((), (), s32[]{:S(2)}) async-start(), calls=%async_computation.2 | async-start | bytes 4325376 | tf_op jit(solution)/shard_map/all_gather | solution.py:26
  26.9 24.6 %copy-start.8 = (f32[1,512]{1,0:T(1,128)}, f32[1,512]{1,0:T(1,128)S(1)}, u32[]{:S(2)}) copy-start(f32[1,512]{1,0:T(1,128)S(1)} %get-tuple-element.3118) | copy-start | bytes 6148
  26.9 24.6 %copy-start.10 = (f32[1,512]{1,0:T(1,128)}, f32[1,512]{1,0:T(1,128)S(1)}, u32[]{:S(2)}) copy-start(f32[1,512]{1,0:T(1,128)S(1)} %get-tuple-element.3119) | copy-start | bytes 6148
  26.9 24.6 %copy-start.12 = (f32[1,512]{1,0:T(1,128)}, f32[1,512]{1,0:T(1,128)S(1)}, u32[]{:S(2)}) copy-start(f32[1,512]{1,0:T(1,128)S(1)} %get-tuple-element.3120) | copy-start | bytes 6148
  26.9 24.6 %copy-start.14 = (f32[1,512]{1,0:T(1,128)}, f32[1,512]{1,0:T(1,128)S(1)}, u32[]{:S(2)}) copy-start(f32[1,512]{1,0:T(1,128)S(1)} %get-tuple-element.3121) | copy-start | bytes 6148
  37.8 11.3 %collective-permute-start = (bf16[3,512]{1,0:T(4,128)(2,1)S(1)}, bf16[3,512]{1,0:T(4,128)(2,1)S(1)}, u32[]{:S(2)}, u32[]{:S(2)}) collective-permute-start(bf16[3,512]{1,0:T(4,128)(2,1)S(1)} %slice.149), channel_id=1, source_target_pairs={{0,16},{16,32},{32,48},{48,64},{64,80},{80,96},{96,112},{112,128},... | collective-permute-start | bytes 9224 | tf_op jit(solution)/shard_map/ppermute | solution.py:21
  50.5 1.8 copy-start.19
  52.3 66.4 %copy-start.5 = (bf16[256,256]{1,0:T(8,128)(2,1)S(1)}, bf16[256,256]{1,0:T(8,128)(2,1)}, u32[]{:S(2)}) copy-start(bf16[256,256]{1,0:T(8,128)(2,1)} %param.27) | copy-start | bytes 393220
  117.9 2.8 copy-start.2
  117.9 2.8 copy-start.3
  118.7 120.8 %all-gather.11.cloned.1.call-start = ((), (), s32[]{:S(2)}) async-start(), calls=%async_computation.3 | async-start | bytes 4325376 | tf_op jit(solution)/shard_map/all_gather | solution.py:26
  130.6 189.0 %all-gather.13.cloned.1.call-start = ((), (), s32[]{:S(2)}) async-start(), calls=%async_computation.4 | async-start | bytes 4325376 | tf_op jit(solution)/shard_map/all_gather | solution.py:26
  131.4 236.1 %all-gather.15.cloned.1.call-start = ((), (), s32[]{:S(2)}) async-start(), calls=%async_computation.5 | async-start | bytes 4325376 | tf_op jit(solution)/shard_map/all_gather | solution.py:26
  319.6 47.9 %copy-start.4 = (f32[2,128,128]{2,1,0:T(8,128)}, f32[2,128,128]{2,1,0:T(8,128)S(1)}, u32[]{:S(2)}) copy-start(f32[2,128,128]{2,1,0:T(8,128)S(1)} %get-tuple-element.2004) | copy-start | bytes 393220
  570.9 29.8 %copy-start.7 = (f32[4,2,64]{2,1,0:T(2,128)S(1)}, f32[4,2,64]{2,1,0:T(2,128)}, u32[]{:S(2)}) copy-start(f32[4,2,64]{2,1,0:T(2,128)} %get-tuple-element.4201) | copy-start | bytes 6148 | tf_op jit(solution)/shard_map/transpose(jvp(vmap()))/while
  570.9 30.1 %copy-start.6 = (f32[4,2,64]{2,1,0:T(2,128)S(1)}, f32[4,2,64]{2,1,0:T(2,128)}, u32[]{:S(2)}) copy-start(f32[4,2,64]{2,1,0:T(2,128)} %get-tuple-element.4198) | copy-start | bytes 6148 | tf_op jit(solution)/shard_map/transpose(jvp(vmap()))/while
  602.8 29.8 %copy-start.7 = (f32[4,2,64]{2,1,0:T(2,128)S(1)}, f32[4,2,64]{2,1,0:T(2,128)}, u32[]{:S(2)}) copy-start(f32[4,2,64]{2,1,0:T(2,128)} %get-tuple-element.4201) | copy-start | bytes 6148 | tf_op jit(solution)/shard_map/transpose(jvp(vmap()))/while
  602.8 30.0 %copy-start.6 = (f32[4,2,64]{2,1,0:T(2,128)S(1)}, f32[4,2,64]{2,1,0:T(2,128)}, u32[]{:S(2)}) copy-start(f32[4,2,64]{2,1,0:T(2,128)} %get-tuple-element.4198) | copy-start | bytes 6148 | tf_op jit(solution)/shard_map/transpose(jvp(vmap()))/while
  634.6 29.8 %copy-start.7 = (f32[4,2,64]{2,1,0:T(2,128)S(1)}, f32[4,2,64]{2,1,0:T(2,128)}, u32[]{:S(2)}) copy-start(f32[4,2,64]{2,1,0:T(2,128)} %get-tuple-element.4201) | copy-start | bytes 6148 | tf_op jit(solution)/shard_map/transpose(jvp(vmap()))/while
  634.6 30.0 %copy-start.6 = (f32[4,2,64]{2,1,0:T(2,128)S(1)}, f32[4,2,64]{2,1,0:T(2,128)}, u32[]{:S(2)}) copy-start(f32[4,2,64]{2,1,0:T(2,128)} %get-tuple-element.4198) | copy-start | bytes 6148 | tf_op jit(solution)/shard_map/transpose(jvp(vmap()))/while
  666.4 29.8 %copy-start.7 = (f32[4,2,64]{2,1,0:T(2,128)S(1)}, f32[4,2,64]{2,1,0:T(2,128)}, u32[]{:S(2)}) copy-start(f32[4,2,64]{2,1,0:T(2,128)} %get-tuple-element.4201) | copy-start | bytes 6148 | tf_op jit(solution)/shard_map/transpose(jvp(vmap()))/while
  666.4 30.1 %copy-start.6 = (f32[4,2,64]{2,1,0:T(2,128)S(1)}, f32[4,2,64]{2,1,0:T(2,128)}, u32[]{:S(2)}) copy-start(f32[4,2,64]{2,1,0:T(2,128)} %get-tuple-element.4198) | copy-start | bytes 6148 | tf_op jit(solution)/shard_map/transpose(jvp(vmap()))/while
  698.3 6.5 copy-start.9
  698.3 6.6 copy-start.11
  698.3 6.6 copy-start.13
  698.3 6.6 copy-start.15
  705.1 17.9 %copy-start.16 = (f32[4,2,64]{2,1,0:T(2,128)S(1)}, f32[4,2,64]{2,1,0:T(2,128)}, u32[]{:S(2)}) copy-start(f32[4,2,64]{2,1,0:T(2,128)} %get-tuple-element.2034) | copy-start | bytes 6148
  705.2 81.1 %copy-start.20 = (f32[2,256]{1,0:T(2,128)S(1)}, f32[2,256]{1,0:T(2,128)}, u32[]{:S(2)}) copy-start(f32[2,256]{1,0:T(2,128)} %param.23) | copy-start | bytes 6148
  705.2 5.0 collective-permute-start.1
  710.9 75.9 %all-to-all-start.1 = ((bf16[16,16,512]{2,1,0:T(8,128)(2,1)}), bf16[16,16,512]{2,1,0:T(8,128)(2,1)S(1)}, u32[]{:S(2)}, u32[]{:S(2)}) async-start(bf16[16,16,512]{2,1,0:T(8,128)(2,1)} %bitcast.32), calls=%async_computation.1 | async-start | bytes 524288 | tf_op jit(solution)/shard_map/all_to_all | solution.py:172
  (3 other events, 2.5 us)
Sparse Core Ops, SparseCore 0:
  118.8 56.0 all-gather.8
  178.6 60.8 all-gather.10
  242.6 60.9 all-gather.12
  306.6 60.8 all-gather.14
where the time goes:
time: 802 us; the launch traced here: 794 us
  matrix products  258 us (32%)
  other arithmetic  180 us (22%)
  waiting for transfers between devices  170 us (21%)
  local copies, waits for them, and re-layouts  64.8 us (8%)
  blocking collectives  62.5 us (8%)
  starting transfers between devices  39.6 us (5%)
  between operations  14.4 us (2%)
    all_gather x4, waiting for transfers between devices, prefix(): everything = jax.tree.map(lambda part: lax.all_gather(part, axis), value)  155 us
    another operation x32, other arithmetic, block_step(): solved = jax.scipy.linalg.solve_triangular(system, right_sides, lower=True)  133 us
    dot_general x64, matrix products, compose(): jnp.einsum('hij,hjk->hik', later[0], earlier[1], precision=highest)  79.4 us
    dot_general x64, matrix products, compose(): matrix = jnp.einsum('hij,hjk->hik', later[0], earlier[0], precision=highest)  75.2 us
    psum x1, blocking collectives, on_device(): weight_total = lax.psum(grad_weight, 'ctx')  62.5 us
    dynamic_update_slice x24, other arithmetic, run_head(): (state_end, transit), outputs = lax.scan(block_step, start, pieces)  18.8 us
    dot_general x16, matrix products, block_step(): scores = ratios * jnp.dot(queries, key_feats.T, precision=highest)  18.5 us
    dot_general x20, matrix products, block_step(): jnp.dot(tail_keys.T, update, precision=highest)  17.8 us
  transfers between devices with their start and end apart: 8, of which 5 were waited for; matrix products, arithmetic and copies ran while one was open for 12% of the time, Pallas kernels for 0%

commit v1 on v0

v1 whole, which is shorter than its diff:
```python
import functools
import jax
import jax.numpy as jnp
from jax import lax
from jax.experimental import pallas as pl
from jax.experimental.pallas import tpu as pltpu
from jax.sharding import PartitionSpec as P

DK = 128
DV = 128
KW = 4
EDGE = 16

f32 = jnp.float32
bf16 = jnp.bfloat16
highest = lax.Precision.HIGHEST
norm_eps = 1e-06


def split(a):
    hi = a.astype(bf16)
    return (hi, (a - hi.astype(f32)).astype(bf16))


def dot(a, b, ca, cb):
    return lax.dot_general(a, b, (((ca,), (cb,)), ((), ())), preferred_element_type=f32)


def mm(a, b, ca=1, cb=0):
    out = dot(a[0], b[0], ca, cb)
    if len(b) > 1:
        out = out + dot(a[0], b[1], ca, cb)
    if len(a) > 1:
        out = out + dot(a[1], b[0], ca, cb)
    return out


def activate(ext, x_ref, edge_ref, w_ref):
    rows = x_ref.shape[0]
    ext[0:EDGE, :] = edge_ref[...].astype(f32)
    ext[EDGE : EDGE + rows, :] = x_ref[...].astype(f32)
    conv = w_ref[KW - 1 : KW, :] * ext[EDGE : EDGE + rows, :]
    for tap in range(KW - 1):
        at = EDGE - (KW - 1) + tap
        conv = conv + w_ref[tap : tap + 1, :] * ext[at : at + rows, :]
    sig = 1.0 / (1.0 + jnp.exp(-conv))
    return conv, sig, conv * sig


def inv_norm(a):
    return lax.rsqrt(jnp.sum(a * a, axis=-1, keepdims=True) + norm_eps)


def gates(logit_ref, g_ref):
    heads, rows = g_ref.shape
    i = lax.broadcasted_iota(jnp.int32, (rows, rows), 0)
    j = lax.broadcasted_iota(jnp.int32, (rows, rows), 1)
    upto = jnp.where(i <= j, 1.0, 0.0).astype(bf16)
    g = g_ref[...]
    g1 = g.astype(bf16)
    rest = g - g1.astype(f32)
    g2 = rest.astype(bf16)
    g3 = (rest - g2.astype(f32)).astype(bf16)
    c_row = (dot(g3, upto, 1, 0) + dot(g2, upto, 1, 0)) + dot(g1, upto, 1, 0)
    b_row = 1.0 / (1.0 + jnp.exp(-logit_ref[...]))
    pad = jnp.zeros((8 - 2 * heads, rows), f32)
    cols = jnp.concatenate([c_row, b_row, pad], axis=0).T
    return c_row, b_row, cols, i, j


def ratios_of(c_col, c_row, i, j):
    return jnp.where(j <= i, jnp.exp(jnp.where(j <= i, c_col - c_row, 0.0)), 0.0)


def invert_unit_lower(low, n):
    i = lax.broadcasted_iota(jnp.int32, (n, n), 0)
    j = lax.broadcasted_iota(jnp.int32, (n, n), 1)
    eye = jnp.where(i == j, 1.0, 0.0)
    inv = [eye - jnp.where((i ^ j) == 1, part, 0.0) for part in low]
    shift = 1
    while (1 << shift) < n:
        pick = ((i >> shift) ^ (j >> shift)) == 1
        parts = [split(a) for a in inv]
        mid = [
            mm(p, split(jnp.where(pick, part, 0.0))) for p, part in zip(parts, low)
        ]
        inv = [a - mm(split(m), p) for a, m, p in zip(inv, mid, parts)]
        shift += 1
    return inv


def prepare_kernel(
    x_ref, edge_ref, w_ref, logit_ref, g_ref, do_ref,
    at_ref, bt_ref, ct_ref, solve_ref, base_ref, weight_ref, score_ref, gram_ref,
    ext,
):
    heads, rows = g_ref.shape
    half = rows // 2
    _, _, act = activate(ext, x_ref, edge_ref, w_ref)
    a, b = act[:, :DK], act[:, DK : 2 * DK]
    q = a * (inv_norm(a) * DK**-0.5)
    k = b * inv_norm(b)
    qs, ks = split(q), split(k)
    gram = mm(ks, ks, 1, 1)
    qk = mm(qs, ks, 1, 1)
    c_row, b_row, cols, i, j = gates(logit_ref, g_ref)
    lows = []
    for h in range(heads):
        ratios = ratios_of(cols[:, h : h + 1], c_row[h : h + 1, :], i, j)
        rg = jnp.where(j < i, ratios * gram, 0.0)
        gram_ref[h] = rg
        score_ref[h] = ratios * qk
        lows.append(cols[:, heads + h : heads + h + 1] * rg)
    diag = []
    for low in lows:
        diag += [low[:half, :half], low[half:, half:]]
    diag = invert_unit_lower(diag, half)
    for h in range(heads):
        first, second = split(diag[2 * h]), split(diag[2 * h + 1])
        corner = mm(split(mm(second, split(lows[h][half:, :half]))), first)
        solve_ref[h, :half, :half] = diag[2 * h]
        solve_ref[h, :half, half:] = jnp.zeros((half, half), f32)
        solve_ref[h, half:, :half] = -corner
        solve_ref[h, half:, half:] = diag[2 * h + 1]
        c_col = cols[:, h : h + 1]
        b_col = cols[:, heads + h : heads + h + 1]
        decays = jnp.exp(c_col)
        last = c_col[rows - 1 : rows, :]
        v = act[:, 2 * DK + h * DV : 2 * DK + (h + 1) * DV]
        right = jnp.concatenate([b_col * v, (b_col * decays) * k], axis=1)
        solved = mm(split(solve_ref[h]), split(right))
        base, weights = solved[:, :DV], solved[:, DV:]
        base_ref[h] = base
        weight_ref[h] = weights
        tail = split(jnp.exp(last - c_col) * k)
        wide = mm(split(solved), tail, 0, 0)
        ii = lax.broadcasted_iota(jnp.int32, (DK, DK), 0)
        jj = lax.broadcasted_iota(jnp.int32, (DK, DK), 1)
        bt_ref[h] = wide[:DV]
        at_ref[h] = jnp.where(ii == jj, jnp.exp(last), 0.0) - wide[DV:]
        reach = decays * q - mm(split(score_ref[h]), split(weights))
        ct_ref[h] = mm((do_ref[:, h * DV : (h + 1) * DV],), split(reach), 0, 0)


def backward_kernel(
    x_ref, edge_ref, w_ref, logit_ref, g_ref, do_ref,
    solve_ref, base_ref, weight_ref, score_ref, gram_ref, st_ref, dst_ref,
    own_ref, last_ref, spill_ref, gw_ref, glogit_ref, gdecay_ref,
    ext, dext,
):
    heads, rows = g_ref.shape
    conv, sig, act = activate(ext, x_ref, edge_ref, w_ref)
    a, b = act[:, :DK], act[:, DK : 2 * DK]
    qr, kr = inv_norm(a), inv_norm(b)
    q = a * (qr * DK**-0.5)
    k = b * kr
    qs, ks = split(q), split(k)
    c_row, b_row, cols, i, j = gates(logit_ref, g_ref)
    lower = j < i
    dq = None
    row_terms, col_terms = [], []
    for h in range(heads):
        c_col = cols[:, h : h + 1]
        b_col = cols[:, heads + h : heads + h + 1]
        decays = jnp.exp(c_col)
        last = c_col[rows - 1 : rows, :]
        tail = jnp.exp(last - c_col)
        ratios = ratios_of(c_col, c_row[h : h + 1, :], i, j)
        v = act[:, 2 * DK + h * DV : 2 * DK + (h + 1) * DV]
        do = do_ref[:, h * DV : (h + 1) * DV]
        st, dst = st_ref[h], dst_ref[h]
        sts, dsts = split(st), split(dst)
        tail_k = tail * k
        update = base_ref[h] - mm(split(weight_ref[h]), sts, 1, 1)
        score = score_ref[h]
        d_update = mm(split(score), (do,), 0, 0) + mm(split(tail_k), dsts, 1, 1)
        x = mm(split(solve_ref[h]), split(d_update), 0, 0)
        us, xs = split(update), split(x)
        d_score = mm((do,), us, 1, 1)
        d_low = -mm(xs, us, 1, 1)
        do_s = mm((do,), sts)
        y = -mm(xs, sts)
        d_tail = mm(us, dsts)
        z = ratios * d_score
        rg = gram_ref[h]
        rgd = rg * d_low
        d_gram = jnp.where(lower, b_col * (ratios * d_low), 0.0)
        part_q = decays * do_s
        part_k = tail * d_tail + (b_col * decays) * y
        if dq is None:
            dq, dk, zs, dgs = part_q, part_k, z, d_gram
        else:
            dq, dk, zs, dgs = dq + part_q, dk + part_k, zs + z, dgs + d_gram
        flow = jnp.where(lower, score * d_score, 0.0) + b_col * rgd
        yk = decays * jnp.sum(y * k, axis=1, keepdims=True)
        tk = jnp.sum(tail_k * d_tail, axis=1, keepdims=True)
        d_beta = (
            jnp.sum(x * v, axis=1, keepdims=True)
            + yk
            + jnp.sum(rgd, axis=1, keepdims=True)
        )
        d_cum = (
            jnp.sum(flow, axis=1, keepdims=True)
            + jnp.sum(q * part_q, axis=1, keepdims=True)
            + b_col * yk
            - tk
        )
        ends = jnp.exp(last) * jnp.sum(dst * st, keepdims=True) + jnp.sum(tk, keepdims=True)
        at_end = lax.broadcasted_iota(jnp.int32, (rows, 1), 0) == rows - 1
        d_cum = d_cum + jnp.where(at_end, ends, 0.0)
        row_terms.append(jnp.sum(flow, axis=0, keepdims=True))
        col_terms.append((d_cum, d_beta))
        s = sig[:, 2 * DK + h * DV : 2 * DK + (h + 1) * DV]
        c = conv[:, 2 * DK + h * DV : 2 * DK + (h + 1) * DV]
        dext[EDGE : EDGE + rows, 2 * DK + h * DV : 2 * DK + (h + 1) * DV] = (
            (b_col * x) * (s * (1.0 + c * (1.0 - s)))
        )
    zs, dgs = split(zs), split(dgs)
    dq = dq + mm(zs, ks)
    dk = dk + mm(zs, qs, 0, 0) + mm(dgs, ks) + mm(dgs, ks, 0, 0)
    for at, value, inv, d, factor in ((0, a, qr, dq, DK**-0.5), (DK, b, kr, dk, 1.0)):
        inner = jnp.sum(value * d, axis=1, keepdims=True)
        d_act = (inv * factor) * (d - value * (inv * inv * inner))
        s, c = sig[:, at : at + DK], conv[:, at : at + DK]
        dext[EDGE : EDGE + rows, at : at + DK] = d_act * (s * (1.0 + c * (1.0 - s)))
    width = dext.shape[1]
    dext[0:EDGE, :] = jnp.zeros((EDGE, width), f32)
    dext[EDGE + rows :, :] = jnp.zeros((dext.shape[0] - EDGE - rows, width), f32)
    own = w_ref[KW - 1 : KW, :] * dext[EDGE : EDGE + rows, :]
    at = EDGE - (EDGE - KW + 1)
    spill = w_ref[KW - 1 : KW, :] * dext[0:EDGE, :]
    for tap in range(KW):
        back = KW - 1 - tap
        if back:
            own = own + w_ref[tap : tap + 1, :] * dext[EDGE + back : EDGE + back + rows, :]
            spill = spill + w_ref[tap : tap + 1, :] * dext[back : back + EDGE, :]
    own_ref[...] = own.astype(bf16)
    last_ref[...] = own[rows - EDGE :, :]
    spill_ref[...] = spill
    d_conv = dext[EDGE : EDGE + rows, :]
    for tap in range(KW):
        at = EDGE - (KW - 1) + tap
        gw_ref[tap : tap + 1, :] = jnp.sum(d_conv * ext[at : at + rows, :], axis=0, keepdims=True)
    lanes = lax.broadcasted_iota(jnp.int32, (rows, 8), 1)
    packed = jnp.zeros((rows, 8), f32)
    for h in range(heads):
        packed = jnp.where(lanes == h, col_terms[h][0], packed)
        packed = jnp.where(lanes == heads + h, col_terms[h][1], packed)
    packed = packed.T
    glogit_ref[...] = packed[heads : 2 * heads] * b_row * (1.0 - b_row)
    d_cum = packed[:heads] - jnp.concatenate(row_terms, axis=0)
    onward = jnp.where(i >= j, 1.0, 0.0).astype(bf16)
    d1 = d_cum.astype(bf16)
    rest = d_cum - d1.astype(f32)
    d2 = rest.astype(bf16)
    d3 = (rest - d2.astype(f32)).astype(bf16)
    gdecay_ref[...] = (dot(d3, onward, 1, 0) + dot(d2, onward, 1, 0)) + dot(d1, onward, 1, 0)


def shape_of(*extent, dtype=f32):
    return jax.ShapeDtypeStruct(extent, dtype)


def prepare(x, edge, w, logits, g, do):
    rows, width = x.shape
    heads = g.shape[0]
    return pl.pallas_call(
        prepare_kernel,
        out_shape=(
            shape_of(heads, DK, DK),
            shape_of(heads, DV, DK),
            shape_of(heads, DV, DK),
            shape_of(heads, rows, rows),
            shape_of(heads, rows, DV),
            shape_of(heads, rows, DK),
            shape_of(heads, rows, rows),
            shape_of(heads, rows, rows),
        ),
        scratch_shapes=[pltpu.VMEM((EDGE + rows, width), f32)],
        compiler_params=pltpu.CompilerParams(vmem_limit_bytes=48 << 20),
        name="prepare",
    )(x, edge, w, logits, g, do)


def backward(x, edge, w, logits, g, do, solve, base, weights, score, gram, st, dst):
    rows, width = x.shape
    heads = g.shape[0]
    return pl.pallas_call(
        backward_kernel,
        out_shape=(
            shape_of(rows, width, dtype=bf16),
            shape_of(EDGE, width),
            shape_of(EDGE, width),
            shape_of(KW, width),
            shape_of(heads, rows),
            shape_of(heads, rows),
        ),
        scratch_shapes=[
            pltpu.VMEM((EDGE + rows, width), f32),
            pltpu.VMEM((2 * EDGE + rows, width), f32),
        ],
        compiler_params=pltpu.CompilerParams(vmem_limit_bytes=48 << 20),
        name="backward",
    )(x, edge, w, logits, g, do, solve, base, weights, score, gram, st, dst)


def from_behind(value, axis, by):
    devices = lax.axis_size(axis)
    pairs = [(i, i + by) for i in range(devices) if 0 <= i + by < devices]
    return lax.ppermute(value, axis, pairs)


def scan_states(at, bt, ct, initial_state, final_state_grad):
    devices, mine = lax.axis_size("ctx"), lax.axis_index("ctx")
    ein = functools.partial(jnp.einsum, precision=highest)

    def sweep(m, o, start, way):
        first = 0 if way > 0 else devices - 1
        o = jnp.where(mine == first, ein("hvi,hij->hvj", start, m) + o, o)
        by = 1
        while by < devices:
            mo, oo = from_behind((m, o), "ctx", way * by)
            has = (mine >= by) if way > 0 else (mine < devices - by)
            o = jnp.where(has, ein("hvi,hij->hvj", oo, m) + o, o)
            m = jnp.where(has, ein("hki,hij->hkj", mo, m), m)
            by *= 2
        return jnp.where(mine == first, start, from_behind(o, "ctx", way))

    st = sweep(at, bt, jnp.swapaxes(initial_state, 1, 2), 1)
    dst = sweep(jnp.swapaxes(at, 1, 2), ct, jnp.swapaxes(final_state_grad, 1, 2), -1)
    return st, dst


def on_device(mixed_in, conv_weight, logits, decay_log, initial_state, final_state_grad, grad_out):
    x = lax.all_to_all(mixed_in, "head", split_axis=1, concat_axis=0, tiled=True)
    edge = from_behind(x[-EDGE:], "ctx", 1)
    at, bt, ct, *kept = prepare(x, edge, conv_weight, logits, decay_log, grad_out)
    st, dst = scan_states(at, bt, ct, initial_state, final_state_grad)
    own, last, spill, gw, glogit, gdecay = backward(
        x, edge, conv_weight, logits, decay_log, grad_out, *kept, st, dst
    )
    last = (last + from_behind(spill, "ctx", -1)).astype(bf16)
    own = jnp.concatenate([own[:-EDGE], last], axis=0)
    returned = lax.all_to_all(own, "head", split_axis=0, concat_axis=1, tiled=True)
    return (returned, lax.psum(gw, "ctx"), glogit, gdecay)


def solution(mesh):
    in_specs = (
        P(("ctx", "head"), None),
        P(None, "head"),
        P("head", "ctx"),
        P("head", "ctx"),
        P("head", None, None),
        P("head", None, None),
        P("ctx", "head"),
    )
    out_specs = (P(("ctx", "head"), None), P(None, "head"), P("head", "ctx"), P("head", "ctx"))
    return jax.shard_map(
        on_device, mesh=mesh, in_specs=in_specs, out_specs=out_specs, check_vma=False
    )
```

time: 802 us -> 208 us (0.26)
  matrix products: 258 us -> 6.75 us
  other arithmetic: 180 us -> 0.76 us
  waiting for transfers between devices: 170 us -> 5.38 us
  local copies, waits for them, and re-layouts: 64.8 us -> 3.6 us
  starting transfers between devices: 39.6 us -> 86.6 us
  blocking collectives: 62.5 us -> 90.9 us
  between operations: 14.4 us -> 1.25 us
  Pallas kernels: 0 us -> 9.93 us
    dot_general x242 -> x20, matrix products: 247 us -> 6.75 us  [the longest x8 3.16 us: sweep(): m = jnp.where(has, ein('hki,hij->hkj', mo, m), m)]
    all_gather x4 -> x0, waiting for transfers between devices: 155 us -> none  [prefix(): everything = jax.tree.map(lambda part: lax.all_gather(part, axis), value)]
    another operation x50 -> x0, other arithmetic: 139 us -> none  [the longest x32 133 us: block_step(): solved = jax.scipy.linalg.solve_triangular(system, right_sides, lower=True)]
    ppermute x2 -> x22, starting transfers between devices: 11.4 us -> 81.1 us  [from_behind(): return lax.ppermute(value, axis, pairs)]
    all_to_all x0 -> x1, blocking collectives: none -> 28.8 us  [on_device(): lax.all_to_all(mixed_in, 'head', split_axis=1, concat_axis=0, tiled=True)]
    all_to_all x2 -> x1, starting transfers between devices: 27.8 us -> 5.51 us  [on_device(): lax.all_to_all(own, 'head', split_axis=0, concat_axis=1, tiled=True)]
    dynamic_update_slice x24 -> x0, other arithmetic: 18.8 us -> none  [run_head(): (state_end, transit), outputs = lax.scan(block_step, start, pieces)]
    another operation x29 -> x0, local copies, waits for them, and re-layouts: 15.7 us -> none
  transfers between devices with their start and end apart: 8 -> 23, of which waited for: 5 -> 2; matrix products, arithmetic and copies ran while one was open for 12% -> 4% of each run, Pallas kernels for 0% -> 0%
where the time goes in v1:
time: 208 us; the launch traced here: 205 us
  blocking collectives  90.9 us (44%)
  starting transfers between devices  86.6 us (42%)
  Pallas kernels  9.93 us (5%)
  matrix products  6.75 us (3%)
  waiting for transfers between devices  5.38 us (3%)
  local copies, waits for them, and re-layouts  3.6 us (2%)
    ppermute x22, starting transfers between devices, from_behind(): return lax.ppermute(value, axis, pairs)  81.1 us
    psum x1, blocking collectives, on_device(): return (returned, lax.psum(gw, 'ctx'), glogit, gdecay)  62 us
    all_to_all x1, blocking collectives, on_device(): lax.all_to_all(mixed_in, 'head', split_axis=1, concat_axis=0, tiled=True)  28.8 us
    all_to_all x1, starting transfers between devices, on_device(): lax.all_to_all(own, 'head', split_axis=0, concat_axis=1, tiled=True)  5.51 us
    pallas_call x1, Pallas kernels, prepare(): pl.pallas_call(prepare_kernel, out_shape=(shape_of(heads, DK, DK), shape_...  5.45 us
    ppermute x22, waiting for transfers between devices, from_behind(): return lax.ppermute(value, axis, pairs)  5.37 us
    pallas_call x1, Pallas kernels, backward(): pl.pallas_call(backward_kernel, out_shape=(shape_of(rows, width, dtype=bf...  4.48 us
  transfers between devices with their start and end apart: 23, of which 2 were waited for; matrix products, arithmetic and copies ran while one was open for 4% of the time, Pallas kernels for 0%

profile of v1, /device:TPU:1, one launch (start us, length us, event | category | flops | bytes accessed | tf_op | source)
XLA Modules:
  0.0 205.1 jit_solution(8964560723994297605)
XLA Ops:
  0.6 1.0 copy.32
  1.6 28.8 %all_to_all.38 = bf16[16,16,512]{2,0,1:T(8,128)(2,1)S(1)} all-to-all(bf16[16,16,512]{2,0,1:T(8,128)(2,1)S(1)} %bitcast.75), channel_id=1, replica_groups=mesh['ctx'=32,'head'=16] {'head'}, dimensions={1} | all-to-all | bytes 524288 | tf_op jit(solution)/shard_map/all_to_all | solution.py:335
  30.4 9.3 %collective-permute-start = (bf16[16,512]{1,0:T(8,128)(2,1)S(1)}, bf16[16,512]{1,0:T(8,128)(2,1)S(1)}, u32[]{:S(2)}, u32[]{:S(2)}) collective-permute-start(bf16[16,512]{1,0:T(8,128)(2,1)S(1)} %slice_bitcast_fusion), channel_id=1, source_target_pairs={{0,16},{16,32},{32,48},{48,64},{64,80},{80,96},{96,112},{112,128},... | collective-permute-start | bytes 49160 | tf_op jit(solution)/shard_map/ppermute | solution.py:310
  39.9 0.8 copy-done.5
  41.6 5.5 %prepare.1 = (f32[2,128,128]{2,1,0:T(8,128)S(1)}, f32[2,128,128]{2,1,0:T(8,128)S(1)}, f32[2,128,128]{2,1,0:T(8,128)S(1)}, f32[2,256,256]{2,1,0:T(8,128)S(1)}, f3...) custom-call(bf16[256,512]{1,0:T(8,128)(2,1)S(1)} %bitcast.72, ...), custom_call_target="tpu_custom_call" | custom-call | tf_op jit(solution)/shard_map/prepare/pallas_call | solution.py:267
  47.0 3.2 %collective-permute-start.3 = (f32[2,128,128]{2,1,0:T(8,128)S(1)}, f32[2,128,128]{2,1,0:T(8,128)}, u32[]{:S(2)}, u32[]{:S(2)}) collective-permute-start(f32[2,128,128]{2,1,0:T(8,128)S(1)} %get-tuple-element.23), channel_id=1, source_target_pairs={{0,16},{16,32},{32,48},{48,64},{64,80},{80,96},{96,112},{112,128},... | collective-permute-start | bytes 393224 | tf_op jit(solution)/shard_map/ppermute | solution.py:310
  50.7 2.3 %collective-permute-start.1 = (f32[2,128,128]{2,1,0:T(8,128)S(1)}, f32[2,128,128]{2,1,0:T(8,128)S(1)}, u32[]{:S(2)}, u32[]{:S(2)}) collective-permute-start(f32[2,128,128]{2,1,0:T(8,128)S(1)} %fusion.1), channel_id=1, source_target_pairs={{0,16},{16,32},{32,48},{48,64},{64,80},{80,96},{96,112},{112,128},... | collective-permute-start | bytes 393224 | tf_op jit(solution)/shard_map/ppermute | solution.py:310
  53.4 2.0 collective-permute-start.11
  55.5 1.9 collective-permute-start.13
  57.7 3.6 %collective-permute-start.2 = (f32[2,128,128]{2,1,0:T(8,128)S(1)}, f32[2,128,128]{2,1,0:T(8,128)S(1)}, u32[]{:S(2)}, u32[]{:S(2)}) collective-permute-start(f32[2,128,128]{2,1,0:T(8,128)S(1)} %fusion.13), channel_id=1, source_target_pairs={{0,32},{16,48},{32,64},{48,80},{64,96},{80,112},{96,128},{112,144}... | collective-permute-start | bytes 393224 | tf_op jit(solution)/shard_map/ppermute | solution.py:310
  61.4 1.2 convolution_select_fusion.6
  62.5 2.9 %collective-permute-start.5 = (f32[2,128,128]{2,1,0:T(8,128)S(1)}, f32[2,128,128]{2,1,0:T(8,128)S(1)}, u32[]{:S(2)}, u32[]{:S(2)}) collective-permute-start(f32[2,128,128]{2,1,0:T(8,128)S(1)} %convolution_select_fusion.6), channel_id=1, source_target_pairs={{0,32},{16,48},{32,64},{48,80},{64,96},{80,112},{96,128},{112,144}... | collective-permute-start | bytes 393224 | tf_op jit(solution)/shard_map/ppermute | solution.py:310
  65.9 1.3 collective-permute-start.12
  67.6 1.3 collective-permute-start.15
  69.1 9.5 %collective-permute-start.4 = (f32[2,128,128]{2,1,0:T(8,128)S(1)}, f32[2,128,128]{2,1,0:T(8,128)S(1)}, u32[]{:S(2)}, u32[]{:S(2)}) collective-permute-start(f32[2,128,128]{2,1,0:T(8,128)S(1)} %fusion.12), channel_id=1, source_target_pairs={{0,64},{16,80},{32,96},{48,112},{64,128},{80,144},{96,160},{112,17... | collective-permute-start | bytes 393224 | tf_op jit(solution)/shard_map/ppermute | solution.py:310
  78.9 6.0 %collective-permute-start.7 = (f32[2,128,128]{2,1,0:T(8,128)S(1)}, f32[2,128,128]{2,1,0:T(8,128)S(1)}, u32[]{:S(2)}, u32[]{:S(2)}) collective-permute-start(f32[2,128,128]{2,1,0:T(8,128)S(1)} %convolution_select_fusion.5), channel_id=1, source_target_pairs={{0,64},{16,80},{32,96},{48,112},{64,128},{80,144},{96,160},{112,17... | collective-permute-start | bytes 393224 | tf_op jit(solution)/shard_map/ppermute | solution.py:310
  85.3 1.3 collective-permute-start.14
  86.8 1.3 collective-permute-start.17
  88.4 7.3 %collective-permute-start.6 = (f32[2,128,128]{2,1,0:T(8,128)S(1)}, f32[2,128,128]{2,1,0:T(8,128)S(1)}, u32[]{:S(2)}, u32[]{:S(2)}) collective-permute-start(f32[2,128,128]{2,1,0:T(8,128)S(1)} %fusion.11), channel_id=1, source_target_pairs={{0,128},{16,144},{32,160},{48,176},{64,192},{80,208},{96,224},{112... | collective-permute-start | bytes 393224 | tf_op jit(solution)/shard_map/ppermute | solution.py:310
  96.0 3.1 %collective-permute-start.9 = (f32[2,128,128]{2,1,0:T(8,128)S(1)}, f32[2,128,128]{2,1,0:T(8,128)S(1)}, u32[]{:S(2)}, u32[]{:S(2)}) collective-permute-start(f32[2,128,128]{2,1,0:T(8,128)S(1)} %convolution_select_fusion.4), channel_id=1, source_target_pairs={{0,128},{16,144},{32,160},{48,176},{64,192},{80,208},{96,224},{112... | collective-permute-start | bytes 393224 | tf_op jit(solution)/shard_map/ppermute | solution.py:310
  99.4 1.3 collective-permute-start.16
  101.0 1.3 collective-permute-start.19
  102.6 6.4 %collective-permute-start.8 = (f32[2,128,128]{2,1,0:T(8,128)S(1)}, f32[2,128,128]{2,1,0:T(8,128)S(1)}, u32[]{:S(2)}, u32[]{:S(2)}) collective-permute-start(f32[2,128,128]{2,1,0:T(8,128)S(1)} %fusion.10), channel_id=1, source_target_pairs={{0,256},{16,272},{32,288},{48,304},{64,320},{80,336},{96,352},{112... | collective-permute-start | bytes 393224 | tf_op jit(solution)/shard_map/ppermute | solution.py:310
  109.3 1.3 collective-permute-start.18
  111.5 6.0 %collective-permute-start.10 = (f32[2,128,128]{2,1,0:T(8,128)S(1)}, f32[2,128,128]{2,1,0:T(8,128)S(1)}, u32[]{:S(2)}, u32[]{:S(2)}) collective-permute-start(f32[2,128,128]{2,1,0:T(8,128)S(1)} %fusion.9), channel_id=1, source_target_pairs={{0,16},{16,32},{32,48},{48,64},{64,80},{80,96},{96,112},{112,128},... | collective-permute-start | bytes 393224 | tf_op jit(solution)/shard_map/ppermute | solution.py:310
  117.8 6.6 %collective-permute-start.20 = (f32[2,128,128]{2,1,0:T(8,128)S(1)}, f32[2,128,128]{2,1,0:T(8,128)S(1)}, u32[]{:S(2)}, u32[]{:S(2)}) collective-permute-start(f32[2,128,128]{2,1,0:T(8,128)S(1)} %fusion.4), channel_id=1, source_target_pairs={{16,0},{32,16},{48,32},{64,48},{80,64},{96,80},{112,96},{128,112},... | collective-permute-start | bytes 393224 | tf_op jit(solution)/shard_map/ppermute | solution.py:310
  124.4 2.0 collective-permute-done.20
  126.4 4.5 %backward.1 = (bf16[256,512]{1,0:T(8,128)(2,1)S(1)}, f32[16,512]{1,0:T(8,128)S(1)}, f32[16,512]{1,0:T(8,128)S(1)}, f32[4,512]{1,0:T(4,128)S(1)}, f32[2,256]{1,0:T(2,128)}, /*index=5*/f32[2,256]{1,0:T(2,128)}) custom-call(bf16[256,512]{1,0:T(8,128)(2,1)S(1)} %bitcast.73, bf16[16,512]{1,0:T(8,128)(2,1)S(1)} %collective-permute-done.edge_ref, ...), custom_call_target="tpu_custom_call" | custom-call | tf_op jit(solution)/shard_map/backward/pallas_call | solution.py:288
  130.9 1.9 collective-permute-start.21
  132.8 3.3 %collective-permute-done.21 = f32[16,512]{1,0:T(8,128)S(1)} collective-permute-done((f32[16,512]{1,0:T(8,128)S(1)}, f32[16,512]{1,0:T(8,128)S(1)}, u32[]{:S(2)}, u32[]{:S(2)}) %collective-permute-start.21) | collective-permute-done | bytes 32800 | tf_op jit(solution)/shard_map/ppermute | solution.py:310
  136.9 5.5 %all-to-all-start.1 = ((bf16[16,16,512]{2,1,0:T(8,128)(2,1)}), bf16[16,16,512]{2,1,0:T(8,128)(2,1)S(1)}, u32[]{:S(2)}, u32[]{:S(2)}) async-start(bf16[16,16,512]{2,1,0:T(8,128)(2,1)} %bitcast.9), calls=%async_computation.1 | async-start | bytes 524288 | tf_op jit(solution)/shard_map/all_to_all | solution.py:344
  142.4 62.0 %psum.7 = f32[4,512]{1,0:T(4,128)} all-reduce(f32[4,512]{1,0:T(4,128)S(1)} %get-tuple-element.29), channel_id=1, replica_groups=mesh['ctx'=32,'head'=16] {'ctx'}, use_global_device_ids=true, to_apply=%region_0.1 | all-reduce | flops 2048 | bytes 16384 | tf_op jit(solution)/shard_map/psum | solution.py:345
  (63 shorter events, 8.2 us)
Async XLA Ops:
  1.6 38.1 %copy-start.4 = (f32[2,128,128]{2,1,0:T(8,128)S(1)}, f32[2,128,128]{2,1,0:T(8,128)}, u32[]{:S(2)}) copy-start(f32[2,128,128]{2,1,0:T(8,128)} %param.11) | copy-start | bytes 393220
  30.4 11.0 %collective-permute-start = (bf16[16,512]{1,0:T(8,128)(2,1)S(1)}, bf16[16,512]{1,0:T(8,128)(2,1)S(1)}, u32[]{:S(2)}, u32[]{:S(2)}) collective-permute-start(bf16[16,512]{1,0:T(8,128)(2,1)S(1)} %slice_bitcast_fusion), channel_id=1, source_target_pairs={{0,16},{16,32},{32,48},{48,64},{64,80},{80,96},{96,112},{112,128},... | collective-permute-start | bytes 49160 | tf_op jit(solution)/shard_map/ppermute | solution.py:310
  39.7 0.9 copy-start.5
  40.6 0.9 copy-start
  40.6 0.9 copy-start.1
  40.6 0.9 copy-start.2
  40.7 0.9 copy-start.3
  47.0 14.3 %collective-permute-start.3 = (f32[2,128,128]{2,1,0:T(8,128)S(1)}, f32[2,128,128]{2,1,0:T(8,128)}, u32[]{:S(2)}, u32[]{:S(2)}) collective-permute-start(f32[2,128,128]{2,1,0:T(8,128)S(1)} %get-tuple-element.23), channel_id=1, source_target_pairs={{0,16},{16,32},{32,48},{48,64},{64,80},{80,96},{96,112},{112,128},... | collective-permute-start | bytes 393224 | tf_op jit(solution)/shard_map/ppermute | solution.py:310
  50.7 6.7 %collective-permute-start.1 = (f32[2,128,128]{2,1,0:T(8,128)S(1)}, f32[2,128,128]{2,1,0:T(8,128)S(1)}, u32[]{:S(2)}, u32[]{:S(2)}) collective-permute-start(f32[2,128,128]{2,1,0:T(8,128)S(1)} %fusion.1), channel_id=1, source_target_pairs={{0,16},{16,32},{32,48},{48,64},{64,80},{80,96},{96,112},{112,128},... | collective-permute-start | bytes 393224 | tf_op jit(solution)/shard_map/ppermute | solution.py:310
  53.4 12.0 %collective-permute-start.11 = (f32[2,128,128]{2,1,0:T(8,128)S(1)}, f32[2,128,128]{2,1,0:T(8,128)S(1)}, u32[]{:S(2)}, u32[]{:S(2)}) collective-permute-start(f32[2,128,128]{2,1,0:T(8,128)S(1)} %fusion.3), channel_id=1, source_target_pairs={{16,0},{32,16},{48,32},{64,48},{80,64},{96,80},{112,96},{128,112},... | collective-permute-start | bytes 393224 | tf_op jit(solution)/shard_map/ppermute | solution.py:310
  55.5 11.7 %collective-permute-start.13 = (f32[2,128,128]{2,1,0:T(8,128)S(1)}, f32[2,128,128]{2,1,0:T(8,128)S(1)}, u32[]{:S(2)}, u32[]{:S(2)}) collective-permute-start(f32[2,128,128]{2,1,0:T(8,128)S(1)} %bitcast.76), channel_id=1, source_target_pairs={{16,0},{32,16},{48,32},{64,48},{80,64},{96,80},{112,96},{128,112},... | collective-permute-start | bytes 393224 | tf_op jit(solution)/shard_map/ppermute | solution.py:310
  57.7 11.2 %collective-permute-start.2 = (f32[2,128,128]{2,1,0:T(8,128)S(1)}, f32[2,128,128]{2,1,0:T(8,128)S(1)}, u32[]{:S(2)}, u32[]{:S(2)}) collective-permute-start(f32[2,128,128]{2,1,0:T(8,128)S(1)} %fusion.13), channel_id=1, source_target_pairs={{0,32},{16,48},{32,64},{48,80},{64,96},{80,112},{96,128},{112,144}... | collective-permute-start | bytes 393224 | tf_op jit(solution)/shard_map/ppermute | solution.py:310
  62.5 16.1 %collective-permute-start.5 = (f32[2,128,128]{2,1,0:T(8,128)S(1)}, f32[2,128,128]{2,1,0:T(8,128)S(1)}, u32[]{:S(2)}, u32[]{:S(2)}) collective-permute-start(f32[2,128,128]{2,1,0:T(8,128)S(1)} %convolution_select_fusion.6), channel_id=1, source_target_pairs={{0,32},{16,48},{32,64},{48,80},{64,96},{80,112},{96,128},{112,144}... | collective-permute-start | bytes 393224 | tf_op jit(solution)/shard_map/ppermute | solution.py:310
  65.9 19.1 %collective-permute-start.12 = (f32[2,128,128]{2,1,0:T(8,128)S(1)}, f32[2,128,128]{2,1,0:T(8,128)S(1)}, u32[]{:S(2)}, u32[]{:S(2)}) collective-permute-start(f32[2,128,128]{2,1,0:T(8,128)S(1)} %fusion.8), channel_id=1, source_target_pairs={{32,0},{48,16},{64,32},{80,48},{96,64},{112,80},{128,96},{144,112}... | collective-permute-start | bytes 393224 | tf_op jit(solution)/shard_map/ppermute | solution.py:310
  67.6 19.0 %collective-permute-start.15 = (f32[2,128,128]{2,1,0:T(8,128)S(1)}, f32[2,128,128]{2,1,0:T(8,128)S(1)}, u32[]{:S(2)}, u32[]{:S(2)}) collective-permute-start(f32[2,128,128]{2,1,0:T(8,128)S(1)} %convolution_select_fusion.7), channel_id=1, source_target_pairs={{32,0},{48,16},{64,32},{80,48},{96,64},{112,80},{128,96},{144,112}... | collective-permute-start | bytes 393224 | tf_op jit(solution)/shard_map/ppermute | solution.py:310
  69.1 19.0 %collective-permute-start.4 = (f32[2,128,128]{2,1,0:T(8,128)S(1)}, f32[2,128,128]{2,1,0:T(8,128)S(1)}, u32[]{:S(2)}, u32[]{:S(2)}) collective-permute-start(f32[2,128,128]{2,1,0:T(8,128)S(1)} %fusion.12), channel_id=1, source_target_pairs={{0,64},{16,80},{32,96},{48,112},{64,128},{80,144},{96,160},{112,17... | collective-permute-start | bytes 393224 | tf_op jit(solution)/shard_map/ppermute | solution.py:310
  78.9 16.8 %collective-permute-start.7 = (f32[2,128,128]{2,1,0:T(8,128)S(1)}, f32[2,128,128]{2,1,0:T(8,128)S(1)}, u32[]{:S(2)}, u32[]{:S(2)}) collective-permute-start(f32[2,128,128]{2,1,0:T(8,128)S(1)} %convolution_select_fusion.5), channel_id=1, source_target_pairs={{0,64},{16,80},{32,96},{48,112},{64,128},{80,144},{96,160},{112,17... | collective-permute-start | bytes 393224 | tf_op jit(solution)/shard_map/ppermute | solution.py:310
  85.3 13.9 %collective-permute-start.14 = (f32[2,128,128]{2,1,0:T(8,128)S(1)}, f32[2,128,128]{2,1,0:T(8,128)S(1)}, u32[]{:S(2)}, u32[]{:S(2)}) collective-permute-start(f32[2,128,128]{2,1,0:T(8,128)S(1)} %fusion.7), channel_id=1, source_target_pairs={{64,0},{80,16},{96,32},{112,48},{128,64},{144,80},{160,96},{176,11... | collective-permute-start | bytes 393224 | tf_op jit(solution)/shard_map/ppermute | solution.py:310
  86.8 13.9 %collective-permute-start.17 = (f32[2,128,128]{2,1,0:T(8,128)S(1)}, f32[2,128,128]{2,1,0:T(8,128)S(1)}, u32[]{:S(2)}, u32[]{:S(2)}) collective-permute-start(f32[2,128,128]{2,1,0:T(8,128)S(1)} %convolution_select_fusion.2), channel_id=1, source_target_pairs={{64,0},{80,16},{96,32},{112,48},{128,64},{144,80},{160,96},{176,11... | collective-permute-start | bytes 393224 | tf_op jit(solution)/shard_map/ppermute | solution.py:310
  88.4 13.9 %collective-permute-start.6 = (f32[2,128,128]{2,1,0:T(8,128)S(1)}, f32[2,128,128]{2,1,0:T(8,128)S(1)}, u32[]{:S(2)}, u32[]{:S(2)}) collective-permute-start(f32[2,128,128]{2,1,0:T(8,128)S(1)} %fusion.11), channel_id=1, source_target_pairs={{0,128},{16,144},{32,160},{48,176},{64,192},{80,208},{96,224},{112... | collective-permute-start | bytes 393224 | tf_op jit(solution)/shard_map/ppermute | solution.py:310
  96.0 14.6 %collective-permute-start.9 = (f32[2,128,128]{2,1,0:T(8,128)S(1)}, f32[2,128,128]{2,1,0:T(8,128)S(1)}, u32[]{:S(2)}, u32[]{:S(2)}) collective-permute-start(f32[2,128,128]{2,1,0:T(8,128)S(1)} %convolution_select_fusion.4), channel_id=1, source_target_pairs={{0,128},{16,144},{32,160},{48,176},{64,192},{80,208},{96,224},{112... | collective-permute-start | bytes 393224 | tf_op jit(solution)/shard_map/ppermute | solution.py:310
  99.4 9.6 %collective-permute-start.16 = (f32[2,128,128]{2,1,0:T(8,128)S(1)}, f32[2,128,128]{2,1,0:T(8,128)S(1)}, u32[]{:S(2)}, u32[]{:S(2)}) collective-permute-start(f32[2,128,128]{2,1,0:T(8,128)S(1)} %fusion.6), channel_id=1, source_target_pairs={{128,0},{144,16},{160,32},{176,48},{192,64},{208,80},{224,96},{240... | collective-permute-start | bytes 393224 | tf_op jit(solution)/shard_map/ppermute | solution.py:310
  101.0 9.9 %collective-permute-start.19 = (f32[2,128,128]{2,1,0:T(8,128)S(1)}, f32[2,128,128]{2,1,0:T(8,128)S(1)}, u32[]{:S(2)}, u32[]{:S(2)}) collective-permute-start(f32[2,128,128]{2,1,0:T(8,128)S(1)} %convolution_select_fusion.1), channel_id=1, source_target_pairs={{128,0},{144,16},{160,32},{176,48},{192,64},{208,80},{224,96},{240... | collective-permute-start | bytes 393224 | tf_op jit(solution)/shard_map/ppermute | solution.py:310
  102.6 8.6 %collective-permute-start.8 = (f32[2,128,128]{2,1,0:T(8,128)S(1)}, f32[2,128,128]{2,1,0:T(8,128)S(1)}, u32[]{:S(2)}, u32[]{:S(2)}) collective-permute-start(f32[2,128,128]{2,1,0:T(8,128)S(1)} %fusion.10), channel_id=1, source_target_pairs={{0,256},{16,272},{32,288},{48,304},{64,320},{80,336},{96,352},{112... | collective-permute-start | bytes 393224 | tf_op jit(solution)/shard_map/ppermute | solution.py:310
  109.3 8.2 %collective-permute-start.18 = (f32[2,128,128]{2,1,0:T(8,128)S(1)}, f32[2,128,128]{2,1,0:T(8,128)S(1)}, u32[]{:S(2)}, u32[]{:S(2)}) collective-permute-start(f32[2,128,128]{2,1,0:T(8,128)S(1)} %fusion.5), channel_id=1, source_target_pairs={{256,0},{272,16},{288,32},{304,48},{320,64},{336,80},{352,96},{368... | collective-permute-start | bytes 393224 | tf_op jit(solution)/shard_map/ppermute | solution.py:310
  111.5 12.9 %collective-permute-start.10 = (f32[2,128,128]{2,1,0:T(8,128)S(1)}, f32[2,128,128]{2,1,0:T(8,128)S(1)}, u32[]{:S(2)}, u32[]{:S(2)}) collective-permute-start(f32[2,128,128]{2,1,0:T(8,128)S(1)} %fusion.9), channel_id=1, source_target_pairs={{0,16},{16,32},{32,48},{48,64},{64,80},{80,96},{96,112},{112,128},... | collective-permute-start | bytes 393224 | tf_op jit(solution)/shard_map/ppermute | solution.py:310
  117.8 8.7 %copy-start.6 = (f32[2,128,128]{1,2,0:T(8,128)S(1)}, f32[2,128,128]{1,2,0:T(8,128)}, u32[]{:S(2)}) copy-start(f32[2,128,128]{1,2,0:T(8,128)} %copy.22) | copy-start | bytes 393220
  117.8 8.6 %collective-permute-start.20 = (f32[2,128,128]{2,1,0:T(8,128)S(1)}, f32[2,128,128]{2,1,0:T(8,128)S(1)}, u32[]{:S(2)}, u32[]{:S(2)}) collective-permute-start(f32[2,128,128]{2,1,0:T(8,128)S(1)} %fusion.4), channel_id=1, source_target_pairs={{16,0},{32,16},{48,32},{64,48},{80,64},{96,80},{112,96},{128,112},... | collective-permute-start | bytes 393224 | tf_op jit(solution)/shard_map/ppermute | solution.py:310
  130.9 5.2 %collective-permute-start.21 = (f32[16,512]{1,0:T(8,128)S(1)}, f32[16,512]{1,0:T(8,128)S(1)}, u32[]{:S(2)}, u32[]{:S(2)}) collective-permute-start(f32[16,512]{1,0:T(8,128)S(1)} %get-tuple-element.28), channel_id=1, source_target_pairs={{16,0},{32,16},{48,32},{64,48},{80,64},{96,80},{112,96},{128,112},... | collective-permute-start | bytes 98312 | tf_op jit(solution)/shard_map/ppermute | solution.py:310
  136.9 67.6 %all-to-all-start.1 = ((bf16[16,16,512]{2,1,0:T(8,128)(2,1)}), bf16[16,16,512]{2,1,0:T(8,128)(2,1)S(1)}, u32[]{:S(2)}, u32[]{:S(2)}) async-start(bf16[16,16,512]{2,1,0:T(8,128)(2,1)} %bitcast.9), calls=%async_computation.1 | async-start | bytes 524288 | tf_op jit(solution)/shard_map/all_to_all | solution.py:344

commit v2 on v1

--- a/solution.py
+++ b/solution.py
@@ -13,7 +13,6 @@
 
 f32 = jnp.float32
 bf16 = jnp.bfloat16
-highest = lax.Precision.HIGHEST
 norm_eps = 1e-06
 
 
@@ -37,7 +36,7 @@
 
 def activate(ext, x_ref, edge_ref, w_ref):
     rows = x_ref.shape[0]
-    ext[0:EDGE, :] = edge_ref[...].astype(f32)
+    ext[0:EDGE, :] = jnp.where(lax.axis_index("ctx") > 0, edge_ref[...].astype(f32), 0.0)
     ext[EDGE : EDGE + rows, :] = x_ref[...].astype(f32)
     conv = w_ref[KW - 1 : KW, :] * ext[EDGE : EDGE + rows, :]
     for tap in range(KW - 1):
@@ -91,7 +90,7 @@
 
 def prepare_kernel(
     x_ref, edge_ref, w_ref, logit_ref, g_ref, do_ref,
-    at_ref, bt_ref, ct_ref, solve_ref, base_ref, weight_ref, score_ref, gram_ref,
+    maps_ref, solve_ref, base_ref, weight_ref, score_ref, gram_ref,
     ext,
 ):
     heads, rows = g_ref.shape
@@ -136,15 +135,15 @@
         wide = mm(split(solved), tail, 0, 0)
         ii = lax.broadcasted_iota(jnp.int32, (DK, DK), 0)
         jj = lax.broadcasted_iota(jnp.int32, (DK, DK), 1)
-        bt_ref[h] = wide[:DV]
-        at_ref[h] = jnp.where(ii == jj, jnp.exp(last), 0.0) - wide[DV:]
+        maps_ref[h, 1] = wide[:DV]
+        maps_ref[h, 0] = jnp.where(ii == jj, jnp.exp(last), 0.0) - wide[DV:]
         reach = decays * q - mm(split(score_ref[h]), split(weights))
-        ct_ref[h] = mm((do_ref[:, h * DV : (h + 1) * DV],), split(reach), 0, 0)
+        maps_ref[h, 2] = mm((do_ref[:, h * DV : (h + 1) * DV],), split(reach), 0, 0)
 
 
 def backward_kernel(
     x_ref, edge_ref, w_ref, logit_ref, g_ref, do_ref,
-    solve_ref, base_ref, weight_ref, score_ref, gram_ref, st_ref, dst_ref,
+    solve_ref, base_ref, weight_ref, score_ref, gram_ref, state_ref,
     own_ref, last_ref, spill_ref, gw_ref, glogit_ref, gdecay_ref,
     ext, dext,
 ):
@@ -168,7 +167,7 @@
         ratios = ratios_of(c_col, c_row[h : h + 1, :], i, j)
         v = act[:, 2 * DK + h * DV : 2 * DK + (h + 1) * DV]
         do = do_ref[:, h * DV : (h + 1) * DV]
-        st, dst = st_ref[h], dst_ref[h]
+        st, dst = state_ref[h, 0], state_ref[h, 1]
         sts, dsts = split(st), split(dst)
         tail_k = tail * k
         update = base_ref[h] - mm(split(weight_ref[h]), sts, 1, 1)
@@ -235,7 +234,7 @@
             own = own + w_ref[tap : tap + 1, :] * dext[EDGE + back : EDGE + back + rows, :]
             spill = spill + w_ref[tap : tap + 1, :] * dext[back : back + EDGE, :]
     own_ref[...] = own.astype(bf16)
-    last_ref[...] = own[rows - EDGE :, :]
+    last_ref[...] = own[rows - last_ref.shape[0] :, :]
     spill_ref[...] = spill
     d_conv = dext[EDGE : EDGE + rows, :]
     for tap in range(KW):
@@ -267,9 +266,7 @@
     return pl.pallas_call(
         prepare_kernel,
         out_shape=(
-            shape_of(heads, DK, DK),
-            shape_of(heads, DV, DK),
-            shape_of(heads, DV, DK),
+            shape_of(heads, 3, DK, DK),
             shape_of(heads, rows, rows),
             shape_of(heads, rows, DV),
             shape_of(heads, rows, DK),
@@ -282,14 +279,14 @@
     )(x, edge, w, logits, g, do)
 
 
-def backward(x, edge, w, logits, g, do, solve, base, weights, score, gram, st, dst):
+def backward(slab, x, edge, w, logits, g, do, solve, base, weights, score, gram, state):
     rows, width = x.shape
     heads = g.shape[0]
     return pl.pallas_call(
         backward_kernel,
         out_shape=(
             shape_of(rows, width, dtype=bf16),
-            shape_of(EDGE, width),
+            shape_of(slab, width),
             shape_of(EDGE, width),
             shape_of(KW, width),
             shape_of(heads, rows),
@@ -301,48 +298,416 @@
         ],
         compiler_params=pltpu.CompilerParams(vmem_limit_bytes=48 << 20),
         name="backward",
-    )(x, edge, w, logits, g, do, solve, base, weights, score, gram, st, dst)
-
-
-def from_behind(value, axis, by):
-    devices = lax.axis_size(axis)
-    pairs = [(i, i + by) for i in range(devices) if 0 <= i + by < devices]
-    return lax.ppermute(value, axis, pairs)
-
-
-def scan_states(at, bt, ct, initial_state, final_state_grad):
-    devices, mine = lax.axis_size("ctx"), lax.axis_index("ctx")
-    ein = functools.partial(jnp.einsum, precision=highest)
-
-    def sweep(m, o, start, way):
-        first = 0 if way > 0 else devices - 1
-        o = jnp.where(mine == first, ein("hvi,hij->hvj", start, m) + o, o)
-        by = 1
-        while by < devices:
-            mo, oo = from_behind((m, o), "ctx", way * by)
-            has = (mine >= by) if way > 0 else (mine < devices - by)
-            o = jnp.where(has, ein("hvi,hij->hvj", oo, m) + o, o)
-            m = jnp.where(has, ein("hki,hij->hkj", mo, m), m)
-            by *= 2
-        return jnp.where(mine == first, start, from_behind(o, "ctx", way))
-
-    st = sweep(at, bt, jnp.swapaxes(initial_state, 1, 2), 1)
-    dst = sweep(jnp.swapaxes(at, 1, 2), ct, jnp.swapaxes(final_state_grad, 1, 2), -1)
-    return st, dst
+    )(x, edge, w, logits, g, do, solve, base, weights, score, gram, state)
+
+
+def ctx_at(i):
+    return {"ctx": i}
+
+
+def head_at(i):
+    return {"head": i}
+
+
+def remote(src, dst, send, recv, device):
+    return pltpu.make_async_remote_copy(
+        src_ref=src,
+        dst_ref=dst,
+        send_sem=send,
+        recv_sem=recv,
+        device_id=device,
+        device_id_type=pl.DeviceIdType.MESH,
+    )
+
+
+def greet(devices):
+    barrier = pltpu.get_barrier_semaphore()
+    for device in devices:
+        pl.semaphore_signal(
+            barrier, inc=1, device_id=device, device_id_type=pl.DeviceIdType.MESH
+        )
+    pl.semaphore_wait(barrier, len(devices))
+
+
+def far_first(n):
+    order = []
+    for d in range(n // 2, 0, -1):
+        order += [d] if 2 * d == n else [d, n - d]
+    return order
+
+
+def gather_kernel(n, nc, x_ref, out_ref, edge_ref, send, recv, edge_send, edge_recv, own_sem):
+    me, c = lax.axis_index("head"), lax.axis_index("ctx")
+    slab, width = x_ref.shape[0], out_ref.shape[1]
+    rows = out_ref.shape[0]
+
+    def slab_at(z):
+        return out_ref.at[pl.ds(pl.multiple_of(z * slab, slab), slab), :]
+
+    def cols(z):
+        return x_ref.at[:, pl.ds(pl.multiple_of(z * width, width), width)]
+
+    after, before = lax.rem(c + 1, nc), lax.rem(c + nc - 1, nc)
+    greet([head_at(lax.rem(me + d, n)) for d in range(1, n)] + [ctx_at(after), ctx_at(before)])
+    own = pltpu.make_async_copy(cols(me), slab_at(me), own_sem)
+    own.start()
+
+    def copy(d):
+        to = lax.rem(me + d, n)
+        return remote(cols(to), slab_at(me), send.at[d], recv.at[d], head_at(to))
+
+    def arriving(d):
+        source = lax.rem(me + n - d, n)
+        return remote(cols(me), slab_at(source), send.at[d], recv.at[d], head_at(source))
+
+    for d in far_first(n):
+        copy(d).start()
+    last = lax.rem(me + 1, n)
+
+    @pl.when(last != 0)
+    def _():
+        arriving(last).wait_recv()
+
+    @pl.when(last == 0)
+    def _():
+        own.wait()
+
+    edge = remote(
+        out_ref.at[pl.ds(rows - EDGE, EDGE), :], edge_ref, edge_send, edge_recv, ctx_at(after)
+    )
+    edge.start()
+
+    @pl.when(last != 0)
+    def _():
+        own.wait()
+
+    for d in range(1, n):
+
+        @pl.when(last != d)
+        def _():
+            arriving(d).wait_recv()
+
+    for d in range(1, n):
+        copy(d).wait_send()
+    edge.wait()
+
+
+def gather_tokens(x):
+    n, nc = lax.axis_size("head"), lax.axis_size("ctx")
+    slab, width = x.shape
+    return pl.pallas_call(
+        functools.partial(gather_kernel, n, nc),
+        out_shape=(
+            shape_of(slab * n, width // n, dtype=bf16),
+            shape_of(EDGE, width // n, dtype=bf16),
+        ),
+        in_specs=[pl.BlockSpec(memory_space=pl.ANY)],
+        out_specs=(pl.BlockSpec(memory_space=pl.ANY), pl.BlockSpec(memory_space=pl.ANY)),
+        scratch_shapes=[
+            pltpu.SemaphoreType.DMA((n,)),
+            pltpu.SemaphoreType.DMA((n,)),
+            pltpu.SemaphoreType.DMA,
+            pltpu.SemaphoreType.DMA,
+            pltpu.SemaphoreType.DMA,
+        ],
+        compiler_params=pltpu.CompilerParams(collective_id=1, has_side_effects=True),
+        name="gather_tokens",
+    )(x)
+
+
+def scan_kernel(
+    chips, maps_ref, first_ref, final_ref, state_ref,
+    sib, start, end, every, cut_out, cut_in, s_out, d_out, s_in, d_in, give,
+    sib_sem, a_send, a_recv, cut_send, cut_recv, s_send, s_recv, d_send, d_recv, give_sem,
+):
+    c = lax.axis_index("ctx")
+    q, k = lax.div(c, 2), lax.rem(c, 2)
+    share = DV // chips
+    sibling = ctx_at(c + 1 - 2 * k)
+
+    def chip(p):
+        return ctx_at(2 * p + k)
+
+    others = [lax.rem(q + d, chips) for d in range(1, chips)]
+    greet([chip(p) for p in others] + [sibling])
+    swap = remote(maps_ref.at[1 - k], sib, sib_sem.at[0], sib_sem.at[1], sibling)
+    swap.start()
+    start[...] = first_ref[k].T
+    end[...] = final_ref[k].T
+    swap.wait_recv()
+    low = k == 0
+    mine = maps_ref[k]
+    theirs = sib[...]
+    a1, b1, c1 = [jnp.where(low, mine[i], theirs[i]) for i in range(3)]
+    a2, b2, c2 = [jnp.where(low, theirs[i], mine[i]) for i in range(3)]
+    a1, a2 = split(a1), split(a2)
+    every[q] = mm(a1, a2)
+    b12 = mm(split(b1), a2) + b2
+    c12 = mm(split(c2), a1, 1, 1) + c1
+    cut_out[:, :share, :] = b12.reshape(chips, share, DK)
+    cut_out[:, share:, :] = c12.reshape(chips, share, DK)
+    order = far_first(chips)
+
+    def a_copy(d):
+        to = lax.rem(q + d, chips)
+        return remote(every.at[q], every.at[q], a_send.at[d], a_recv.at[q], chip(to))
+
+    def cut_copy(d):
+        to = lax.rem(q + d, chips)
+        return remote(cut_out.at[to], cut_in.at[q], cut_send.at[d], cut_recv.at[q], chip(to))
+
+    for d in order:
+        cut_copy(d).start()
+        a_copy(d).start()
+    cut_in[q] = cut_out[q]
+    my_rows = pl.ds(pl.multiple_of(q * share, share), share)
+    s, d = start[my_rows, :], end[my_rows, :]
+    here = set()
+
+    def arrive(p):
+        if p in here:
+            return
+        here.add(p)
+
+        @pl.when(q != p)
+        def _():
+            remote(every.at[q], every.at[p], a_send.at[0], a_recv.at[p], chip(p)).wait_recv()
+            remote(cut_out.at[p], cut_in.at[p], cut_send.at[0], cut_recv.at[p], chip(p)).wait_recv()
+
+    def hand_out(p, value, out, into, send, recv):
+        out[p] = value
+
+        @pl.when(q != p)
+        def _():
+            remote(out.at[p], into.at[my_rows, :], send.at[p], recv.at[q], chip(p)).start()
+
+        @pl.when(q == p)
+        def _():
+            into[my_rows, :] = value
+
+    for t in range(chips):
+        u = chips - 1 - t
+        hand_out(t, s, s_out, s_in, s_send, s_recv)
+        hand_out(u, d, d_out, d_in, d_send, d_recv)
+        if t < chips - 1:
+            arrive(t)
+            arrive(u)
+            s = mm(split(s), split(every[t])) + cut_in[t, :share, :]
+            d = mm(split(d), split(every[u]), 1, 1) + cut_in[u, share:, :]
+
+    def finish(p, out, into, send, recv):
+        rows = pl.ds(p * share, share)
+
+        @pl.when(q != p)
+        def _():
+            copy = remote(out.at[p], into.at[rows, :], send.at[p], recv.at[p], chip(p))
+            copy.wait_recv()
+            copy.wait_send()
+
+    for p in range(chips):
+        finish(p, s_out, s_in, s_send, s_recv)
+        finish(p, d_out, d_in, d_send, d_recv)
+    s, d = s_in[...], d_in[...]
+    s2 = mm(split(s), a1) + b1
+    d1 = mm(split(d), a2, 1, 1) + c2
+    give[0] = jnp.where(low, s2, s)
+    give[1] = jnp.where(low, d, d1)
+    pass_on = remote(give, state_ref.at[k], give_sem.at[0], give_sem.at[1], sibling)
+    pass_on.start()
+    state_ref[k, 0] = jnp.where(low, s, s2)
+    state_ref[k, 1] = jnp.where(low, d1, d)
+    swap.wait_send()
+    for d in range(1, chips):
+        a_copy(d).wait_send()
+        cut_copy(d).wait_send()
+    pass_on.wait()
+
+
+def scan_states(maps, initial_state, final_state_grad):
+    chips = lax.axis_size("ctx") // 2
+    heads = maps.shape[0]
+    share = DV // chips
+    sems = pltpu.SemaphoreType.DMA
+    whole = pl.BlockSpec(memory_space=pltpu.VMEM)
+    return pl.pallas_call(
+        functools.partial(scan_kernel, chips),
+        out_shape=shape_of(heads, 2, DV, DK),
+        in_specs=[whole] * 3,
+        out_specs=whole,
+        scratch_shapes=[
+            pltpu.VMEM((3, DK, DK), f32),
+            pltpu.VMEM((DV, DK), f32),
+            pltpu.VMEM((DV, DK), f32),
+            pltpu.VMEM((chips, DK, DK), f32),
+            pltpu.VMEM((chips, 2 * share, DK), f32),
+            pltpu.VMEM((chips, 2 * share, DK), f32),
+            pltpu.VMEM((chips, share, DK), f32),
+            pltpu.VMEM((chips, share, DK), f32),
+            pltpu.VMEM((DV, DK), f32),
+            pltpu.VMEM((DV, DK), f32),
+            pltpu.VMEM((2, DV, DK), f32),
+            sems((2,)),
+            sems((chips,)),
+            sems((chips,)),
+            sems((chips,)),
+            sems((chips,)),
+            sems((chips,)),
+            sems((chips,)),
+            sems((chips,)),
+            sems((chips,)),
+            sems((2,)),
+        ],
+        compiler_params=pltpu.CompilerParams(collective_id=2, has_side_effects=True),
+        name="scan_states",
+    )(maps, initial_state, final_state_grad)
+
+
+def return_kernel(
+    n, nc, near, own_ref, last_ref, spill_ref, gw_ref, out_ref, total_ref,
+    final, inbox, near_sums, far_sums,
+    send, recv, own_sem, spill_sem, near_send, near_recv, far_send, far_recv,
+):
+    me, c = lax.axis_index("head"), lax.axis_index("ctx")
+    slab = out_ref.shape[0]
+    width = own_ref.shape[1]
+    g, r = lax.div(c, near), lax.rem(c, near)
+    far = nc // near
+    after, before = lax.rem(c + 1, nc), lax.rem(c + nc - 1, nc)
+
+    def near_at(d):
+        return ctx_at(g * near + lax.rem(r + d, near))
+
+    def far_at(d):
+        return ctx_at(lax.rem(g + d, far) * near + r)
+
+    greet(
+        [head_at(lax.rem(me + d, n)) for d in range(1, n)]
+        + [ctx_at(after), ctx_at(before)]
+        + [near_at(d) for d in range(1, near)]
+        + [far_at(d) for d in range(1, far)]
+    )
+    spilled = remote(spill_ref, inbox, spill_sem.at[0], spill_sem.at[1], ctx_at(before))
+    spilled.start()
+    near_sums[r] = gw_ref[...]
+
+    def near_copy(d):
+        return remote(near_sums.at[r], near_sums.at[r], near_send.at[d], near_recv.at[r], near_at(d))
+
+    def far_copy(d):
+        return remote(far_sums.at[g], far_sums.at[g], far_send.at[d], far_recv.at[g], far_at(d))
+
+    for d in range(1, near):
+        near_copy(d).start()
+
+    def slab_at(z):
+        return own_ref.at[pl.ds(pl.multiple_of(z * slab, slab), slab), :]
+
+    def cols(z):
+        return out_ref.at[:, pl.ds(pl.multiple_of(z * width, width), width)]
+
+    def copy(d, source=None):
+        to = lax.rem(me + d, n)
+        source = slab_at(to) if source is None else source
+        return remote(source, cols(me), send.at[d], recv.at[d], head_at(to))
+
+    for d in far_first(n):
+
+        @pl.when(lax.rem(me + d, n) != n - 1)
+        def _():
+            copy(d).start()
+
+    own = pltpu.make_async_copy(slab_at(me), cols(me), own_sem)
+    own_last = pltpu.make_async_copy(final, cols(me), own_sem)
+
+    @pl.when(me != n - 1)
+    def _():
+        own.start()
+
+    spilled.wait()
+    final[...] = last_ref[...].astype(bf16)
+    more = jnp.where(c < nc - 1, inbox[...], 0.0)
+    final[slab - EDGE :, :] = (last_ref[slab - EDGE :, :] + more).astype(bf16)
+    last = lax.rem(2 * n - 1 - me, n)
+
+    @pl.when(me != n - 1)
+    def _():
+        copy(last, final).start()
+
+    @pl.when(me == n - 1)
+    def _():
+        own_last.start()
+
+    for d in range(1, near):
+        source = lax.rem(r + near - d, near)
+        remote(
+            near_sums.at[r], near_sums.at[source], near_send.at[d], near_recv.at[source], near_at(d)
+        ).wait_recv()
+    total = near_sums[0]
+    for i in range(1, near):
+        total = total + near_sums[i]
+    far_sums[g] = total
+    for d in range(1, far):
+        far_copy(d).start()
+    for d in range(1, far):
+        source = lax.rem(g + far - d, far)
+        remote(
+            far_sums.at[g], far_sums.at[source], far_send.at[d], far_recv.at[source], far_at(d)
+        ).wait_recv()
+    total = far_sums[0]
+    for i in range(1, far):
+        total = total + far_sums[i]
+    total_ref[...] = total
+    for d in range(1, near):
+        near_copy(d).wait_send()
+    for d in range(1, far):
+        far_copy(d).wait_send()
+    for d in range(1, n):
+        source = lax.rem(me + n - d, n)
+        remote(slab_at(me), cols(source), send.at[d], recv.at[d], head_at(source)).wait_recv()
+        copy(d, final).wait_send()
+    own_last.wait()
+
+
+def return_tokens(own, last, spill, gw):
+    n, nc = lax.axis_size("head"), lax.axis_size("ctx")
+    near = 8
+    rows, width = own.shape
+    sems = pltpu.SemaphoreType.DMA
+    whole = pl.BlockSpec(memory_space=pltpu.VMEM)
+    anywhere = pl.BlockSpec(memory_space=pl.ANY)
+    return pl.pallas_call(
+        functools.partial(return_kernel, n, nc, near),
+        out_shape=(shape_of(rows // n, width * n, dtype=bf16), shape_of(*gw.shape)),
+        in_specs=[anywhere, whole, whole, whole],
+        out_specs=(anywhere, whole),
+        scratch_shapes=[
+            pltpu.VMEM((rows // n, width), bf16),
+            pltpu.VMEM(spill.shape, f32),
+            pltpu.VMEM((near, *gw.shape), f32),
+            pltpu.VMEM((nc // near, *gw.shape), f32),
+            sems((n,)),
+            sems((n,)),
+            sems,
+            sems((2,)),
+            sems((near,)),
+            sems((near,)),
+            sems((nc // near,)),
+            sems((nc // near,)),
+        ],
+        compiler_params=pltpu.CompilerParams(collective_id=3, has_side_effects=True),
+        name="return_tokens",
+    )(own, last, spill, gw)
 
 
 def on_device(mixed_in, conv_weight, logits, decay_log, initial_state, final_state_grad, grad_out):
-    x = lax.all_to_all(mixed_in, "head", split_axis=1, concat_axis=0, tiled=True)
-    edge = from_behind(x[-EDGE:], "ctx", 1)
-    at, bt, ct, *kept = prepare(x, edge, conv_weight, logits, decay_log, grad_out)
-    st, dst = scan_states(at, bt, ct, initial_state, final_state_grad)
+    x, edge = gather_tokens(mixed_in)
+    maps, *kept = prepare(x, edge, conv_weight, logits, decay_log, grad_out)
+    state = scan_states(maps, initial_state, final_state_grad)
     own, last, spill, gw, glogit, gdecay = backward(
-        x, edge, conv_weight, logits, decay_log, grad_out, *kept, st, dst
+        mixed_in.shape[0], x, edge, conv_weight, logits, decay_log, grad_out, *kept, state
     )
-    last = (last + from_behind(spill, "ctx", -1)).astype(bf16)
-    own = jnp.concatenate([own[:-EDGE], last], axis=0)
-    returned = lax.all_to_all(own, "head", split_axis=0, concat_axis=1, tiled=True)
-    return (returned, lax.psum(gw, "ctx"), glogit, gdecay)
+    returned, total = return_tokens(own, last, spill, gw)
+    return (returned, total, glogit, gdecay)
 
 
 def solution(mesh):

time: 208 us -> 109 us (0.52)
  blocking collectives: 90.9 us -> 0 us
  Pallas kernels: 9.93 us -> 98.5 us
  starting transfers between devices: 86.6 us -> 0 us
  matrix products: 6.75 us -> 0 us
  waiting for transfers between devices: 5.38 us -> 0 us
  local copies, waits for them, and re-layouts: 3.6 us -> 8.83 us
    pallas_call x1 -> x4, Pallas kernels: 5.45 us -> 94.1 us  [the longest x1 38.3 us: scan_states(): pl.pallas_call(functools.partial(scan_kernel, chips), out_shape=shape_of(...]
    ppermute x22 -> x0, starting transfers between devices: 81.1 us -> none  [from_behind(): return lax.ppermute(value, axis, pairs)]
    psum x1 -> x0, blocking collectives: 62 us -> none  [on_device(): return (returned, lax.psum(gw, 'ctx'), glogit, gdecay)]
    all_to_all x1 -> x0, blocking collectives: 28.8 us -> none  [on_device(): lax.all_to_all(mixed_in, 'head', split_axis=1, concat_axis=0, tiled=True)]
    unnamed x16 -> x32, local copies, waits for them, and re-layouts: 1.8 us -> 8.83 us
    dot_general x20 -> x0, matrix products: 6.75 us -> none  [the longest x8 3.16 us: sweep(): m = jnp.where(has, ein('hki,hij->hkj', mo, m), m)]
    all_to_all x1 -> x0, starting transfers between devices: 5.51 us -> none  [on_device(): lax.all_to_all(own, 'head', split_axis=0, concat_axis=1, tiled=True)]
    ppermute x22 -> x0, waiting for transfers between devices: 5.37 us -> none  [from_behind(): return lax.ppermute(value, axis, pairs)]
  transfers between devices with their start and end apart: 23 -> 0, of which waited for: 2 -> 0; matrix products, arithmetic and copies ran while one was open for 4% -> 0% of each run, Pallas kernels for 0% -> 0%
where the time goes in v2:
time: 109 us; the launch traced here: 108 us
  Pallas kernels  98.5 us (90%)
  local copies, waits for them, and re-layouts  8.83 us (8%)
    pallas_call x1, Pallas kernels, scan_states(): pl.pallas_call(functools.partial(scan_kernel, chips), out_shape=shape_of(...  38.3 us
    pallas_call x1, Pallas kernels, gather_tokens(): pl.pallas_call(functools.partial(gather_kernel, n, nc), out_shape=(shape_...  30.1 us
    pallas_call x1, Pallas kernels, return_tokens(): pl.pallas_call(functools.partial(return_kernel, n, nc, near), out_shape=(...  20.2 us
    unnamed x32, local copies, waits for them, and re-layouts  8.83 us
    pallas_call x1, Pallas kernels, prepare(): pl.pallas_call(prepare_kernel, out_shape=(shape_of(heads, 3, DK, DK), sha...  5.45 us
    pallas_call x1, Pallas kernels, backward(): pl.pallas_call(backward_kernel, out_shape=(shape_of(rows, width, dtype=bf...  4.47 us

profile of v2, /device:TPU:1, one launch (start us, length us, event | category | flops | bytes accessed | tf_op | source)
XLA Modules:
  0.0 108.1 jit_solution(6070908043833515737)
XLA Ops:
  0.6 0.0 copy-start.3
  0.6 0.0 copy-start.8
  0.7 0.0 copy-start.13
  0.7 30.1 %gather_tokens.1 = (bf16[256,512]{1,0:T(8,128)(2,1)}, bf16[16,512]{1,0:T(8,128)(2,1)}) custom-call(bf16[16,8192]{1,0:T(8,128)(2,1)} %x_ref.1), custom_call_target="tpu_custom_call" | custom-call | tf_op jit(solution)/shard_map/gather_tokens/pallas_call | solution.py:398
  30.7 0.0 copy-start.12
  30.7 0.0 copy-done.3
  30.7 0.0 copy-done.8
  30.8 0.0 copy-done.13
  30.8 0.6 copy-done.12
  31.4 0.0 copy-start.1
  31.4 0.9 copy-done.1
  32.4 0.0 copy-start.6
  32.4 0.7 copy-done.6
  33.1 5.4 %prepare.1 = (f32[2,3,128,128]{3,2,1,0:T(8,128)S(1)}, f32[2,256,256]{2,1,0:T(8,128)S(1)}, f32[2,256,128]{2,1,0:T(8,128)S(1)}, f32[2,256,128]{2,1,0:T(8,128)S(1)}...) custom-call(bf16[256,512]{1,0:T(8,128)(2,1)S(1)} %copy-done.1, bf16[16,512]{1,0:T(8,128)(2,1)S(1)} %copy-done.6, ...), custom_call_target="tpu_custom_call" | custom-call | tf_op jit(solution)/shard_map/prepare/pallas_call | solution.py:266
  38.5 0.0 copy-start.4
  38.5 0.7 copy-done.4
  39.3 0.0 copy-start.2
  39.3 38.3 %scan_states.1.state_ref = f32[2,2,128,128]{3,2,1,0:T(8,128)} custom-call(f32[2,3,128,128]{3,2,1,0:T(8,128)} %copy-done.4, f32[2,128,128]{2,1,0:T(8,128)} %first_ref.1, f32[2,128,128]{2,1,0:T(8,128)} %final_ref.1), custom_call_target="tpu_custom_call" | custom-call | tf_op jit(solution)/shard_map/scan_states/pallas_call | solution.py:532
  77.6 0.0 copy-done.2
  77.6 0.0 copy-done.7
  77.7 0.0 copy-start
  77.7 0.9 copy-done
  78.6 4.5 %backward.1 = (bf16[256,512]{1,0:T(8,128)(2,1)S(1)}, f32[16,512]{1,0:T(8,128)S(1)}, f32[16,512]{1,0:T(8,128)S(1)}, f32[4,512]{1,0:T(4,128)S(1)}, f32[2,256]{1,0:T(2,128)}, /*index=5*/f32[2,256]{1,0:T(2,128)}) custom-call(bf16[256,512]{1,0:T(8,128)(2,1)S(1)} %copy-done.2, bf16[16,512]{1,0:T(8,128)(2,1)S(1)} %copy-done.7, f32[4,512]{1,0:T(4,128)S(1)} %copy-done.8, ...), custom_call_target="tpu_custom_call" | custom-call | tf_op jit(solution)/shard_map/backward/pallas_call | solution.py:285
  83.1 0.7 copy-done.5
  83.8 0.6 copy-done.9
  84.4 0.6 copy-done.10
  85.0 0.6 copy-done.11
  85.6 20.2 %return_tokens.1 = (bf16[16,8192]{1,0:T(8,128)(2,1)}, f32[4,512]{1,0:T(4,128)}) custom-call(bf16[256,512]{1,0:T(8,128)(2,1)} %copy-done.5, f32[16,512]{1,0:T(8,128)} %copy-done.9, f32[16,512]{1,0:T(8,128)} %copy-done.10, f32[4,512]{1,0:T(4,128)} %copy-done.11), custom_call_target="tpu_custom_call" | custom-call | tf_op jit(solution)/shard_map/return_tokens/pallas_call | solution.py:678
  105.8 0.0 copy-start.14
  105.9 1.7 %copy.13 = bf16[16,8192]{1,0:T(8,128)(2,1)} copy(bf16[16,8192]{1,0:T(8,128)(2,1)} %get-tuple-element.40) | data formatting | bytes 524288
  107.5 0.0 copy-done.14
  107.5 0.6 copy.14
  (5 shorter events, 0.0 us)
Async XLA Ops:
  0.6 30.1 %copy-start.3 = (bf16[256,256]{1,0:T(8,128)(2,1)S(1)}, bf16[256,256]{1,0:T(8,128)(2,1)}, u32[]{:S(2)}) copy-start(bf16[256,256]{1,0:T(8,128)(2,1)} %do_ref.3) | copy-start | bytes 393220
  0.6 30.1 %copy-start.8 = (f32[4,512]{1,0:T(4,128)S(1)}, f32[4,512]{1,0:T(4,128)}, u32[]{:S(2)}) copy-start(f32[4,512]{1,0:T(4,128)} %w_ref.3) | copy-start | bytes 24580
  0.7 30.1 %copy-start.13 = (f32[2,256]{1,0:T(2,128)S(1)}, f32[2,256]{1,0:T(2,128)}, u32[]{:S(2)}) copy-start(f32[2,256]{1,0:T(2,128)} %g_ref.3) | copy-start | bytes 6148
  30.7 0.7 copy-start.12
  31.4 0.9 copy-start.1
  32.4 0.7 copy-start.6
  38.5 0.8 copy-start.4
  39.3 38.3 %copy-start.2 = (bf16[256,512]{1,0:T(8,128)(2,1)S(1)}, bf16[256,512]{1,0:T(8,128)(2,1)}, u32[]{:S(2)}) copy-start(bf16[256,512]{1,0:T(8,128)(2,1)} %get-tuple-element.20.x_ref) | copy-start | bytes 786436
  39.3 38.4 %copy-start.7 = (bf16[16,512]{1,0:T(8,128)(2,1)S(1)}, bf16[16,512]{1,0:T(8,128)(2,1)}, u32[]{:S(2)}) copy-start(bf16[16,512]{1,0:T(8,128)(2,1)} %get-tuple-element.21.edge_ref) | copy-start | bytes 49156
  77.7 1.0 copy-start
  83.1 0.7 copy-start.5
  83.8 0.6 copy-start.9
  84.4 0.6 copy-start.10
  85.0 0.6 copy-start.11
  105.8 1.7 %copy-start.14 = (f32[4,512]{1,0:T(4,128)S(1)}, f32[4,512]{1,0:T(4,128)}, u32[]{:S(2)}) copy-start(f32[4,512]{1,0:T(4,128)} %get-tuple-element.41) | copy-start | bytes 24580

commit v3 on v1

v3 whole, which is shorter than its diff:
```python
import functools
import jax
import jax.numpy as jnp
from jax import lax
from jax.experimental import pallas as pl
from jax.experimental.pallas import tpu as pltpu
from jax.sharding import PartitionSpec as P

DK = 128
DV = 128
KW = 4
EDGE = 16

f32 = jnp.float32
bf16 = jnp.bfloat16
norm_eps = 1e-06


def split(a):
    hi = a.astype(bf16)
    return (hi, (a - hi.astype(f32)).astype(bf16))


def dot(a, b, ca, cb):
    return lax.dot_general(a, b, (((ca,), (cb,)), ((), ())), preferred_element_type=f32)


def mm(a, b, ca=1, cb=0):
    out = dot(a[0], b[0], ca, cb)
    if len(b) > 1:
        out = out + dot(a[0], b[1], ca, cb)
    if len(a) > 1:
        out = out + dot(a[1], b[0], ca, cb)
    return out


def inv_norm(a):
    return lax.rsqrt(jnp.sum(a * a, axis=-1, keepdims=True) + norm_eps)


def gates(logit_ref, g_ref):
    heads, rows = g_ref.shape
    i = lax.broadcasted_iota(jnp.int32, (rows, rows), 0)
    j = lax.broadcasted_iota(jnp.int32, (rows, rows), 1)
    upto = jnp.where(i <= j, 1.0, 0.0).astype(bf16)
    g = g_ref[...]
    g1 = g.astype(bf16)
    rest = g - g1.astype(f32)
    g2 = rest.astype(bf16)
    g3 = (rest - g2.astype(f32)).astype(bf16)
    c_row = (dot(g3, upto, 1, 0) + dot(g2, upto, 1, 0)) + dot(g1, upto, 1, 0)
    b_row = 1.0 / (1.0 + jnp.exp(-logit_ref[...]))
    pad = jnp.zeros((8 - 2 * heads, rows), f32)
    cols = jnp.concatenate([c_row, b_row, pad], axis=0).T
    return c_row, b_row, cols, i, j


def ratios_of(c_col, c_row, i, j):
    return jnp.where(j <= i, jnp.exp(jnp.where(j <= i, c_col - c_row, 0.0)), 0.0)


def invert_unit_lower(low, n):
    i = lax.broadcasted_iota(jnp.int32, (n, n), 0)
    j = lax.broadcasted_iota(jnp.int32, (n, n), 1)
    eye = jnp.where(i == j, 1.0, 0.0)
    inv = [eye - jnp.where((i ^ j) == 1, part, 0.0) for part in low]
    shift = 1
    while (1 << shift) < n:
        pick = ((i >> shift) ^ (j >> shift)) == 1
        parts = [split(a) for a in inv]
        mid = [
            mm(p, split(jnp.where(pick, part, 0.0))) for p, part in zip(parts, low)
        ]
        inv = [a - mm(split(m), p) for a, m, p in zip(inv, mid, parts)]
        shift += 1
    return inv


def shape_of(*extent, dtype=f32):
    return jax.ShapeDtypeStruct(extent, dtype)


def ctx_at(i):
    return {"ctx": i}


def head_at(i):
    return {"head": i}


def remote(src, dst, send, recv, device):
    return pltpu.make_async_remote_copy(
        src_ref=src,
        dst_ref=dst,
        send_sem=send,
        recv_sem=recv,
        device_id=device,
        device_id_type=pl.DeviceIdType.MESH,
    )


def greet(devices):
    barrier = pltpu.get_barrier_semaphore()
    for device in devices:
        pl.semaphore_signal(
            barrier, inc=1, device_id=device, device_id_type=pl.DeviceIdType.MESH
        )
    pl.semaphore_wait(barrier, len(devices))


def far_first(n):
    order = []
    for d in range(n // 2, 0, -1):
        order += [d] if 2 * d == n else [d, n - d]
    return order


def layer_kernel(
    n, nc, x_hbm, w_hbm, logit_hbm, g_hbm, do_hbm, first_hbm, final_hbm,
    out_hbm, total_hbm, glogit_hbm, gdecay_hbm,
    w_ref, logit_ref, g_ref, do_ref, start, end,
    x_in, edge, ext, dext, conv_ref, sig_ref, qk_ref,
    ratio_ref, gram_ref, score_ref, solve_ref, base_ref, weight_ref, push_ref,
    a_mine, bc_mine, a_sib, bc_sib, every, cut_out, cut_in,
    s_out, d_out, s_in, d_in, give, state_ref,
    own_ref, tail_ref, spill_ref, inbox, last_ref,
    gw_ref, gw_sib, gw_all, total_ref, glogit_ref, gdecay_ref,
    load_sem, store_sem, own_sem, x_send, x_recv, edge_send, edge_recv, swap_send, swap_recv,
    a_send, a_recv, cut_send, cut_recv, s_send, s_recv, d_send, d_recv,
    spill_send, spill_recv, back_send, back_recv, gw_send, gw_recv,
):
    me, c = lax.axis_index("head"), lax.axis_index("ctx")
    heads, rows = g_ref.shape
    slab, width = x_hbm.shape[0], x_in.shape[1]
    half = rows // 2
    chips = nc // 2
    share = DV // chips
    q_at, k_at = lax.div(c, 2), lax.rem(c, 2)
    low = k_at == 0
    after, before = lax.rem(c + 1, nc), lax.rem(c + nc - 1, nc)
    sibling = ctx_at(c + 1 - 2 * k_at)
    other = ctx_at(lax.rem(c + nc - 1 + 2 * k_at, nc))

    def chip(p):
        return ctx_at(2 * p + k_at)

    def chip_off(d):
        return lax.rem(q_at + d, chips)

    loads = [
        pltpu.make_async_copy(source, target, load_sem.at[i])
        for i, (source, target) in enumerate(
            (
                (logit_hbm, logit_ref),
                (g_hbm, g_ref),
                (w_hbm, w_ref),
                (do_hbm, do_ref),
                (first_hbm.at[k_at], start),
                (final_hbm.at[k_at], end),
            )
        )
    ]
    for load in loads:
        load.start()

    def slab_at(z):
        return x_in.at[pl.ds(pl.multiple_of(z * slab, slab), slab), :]

    def cols(z, at=0, size=width):
        return pl.ds(pl.multiple_of(z * width + at, 128), size)

    own = pltpu.make_async_copy(x_hbm.at[:, cols(me)], slab_at(me), own_sem)
    own.start()
    greet(
        [head_at(lax.rem(me + d, n)) for d in far_first(n)]
        + [chip(chip_off(d)) for d in far_first(chips)]
        + [sibling, other]
    )

    parts = ((DK, DK), (0, DK), (2 * DK, heads * DV))

    def send_x(i, d):
        at, size = parts[i]
        to = lax.rem(me + d, n)
        return remote(
            x_hbm.at[:, cols(to, at, size)],
            slab_at(me).at[:, pl.ds(at, size)],
            x_send.at[i, d], x_recv.at[i, d], head_at(to),
        )

    def take_x(i, d):
        at, size = parts[i]
        source = lax.rem(me + n - d, n)
        remote(
            x_hbm.at[:, cols(me, at, size)],
            slab_at(source).at[:, pl.ds(at, size)],
            x_send.at[i, d], x_recv.at[i, d], head_at(source),
        ).wait_recv()

    for i in range(3):
        for d in far_first(n):
            send_x(i, d).start()

    def send_edge(i):
        at, size = parts[i]
        return remote(
            x_in.at[pl.ds(rows - EDGE, EDGE), pl.ds(at, size)],
            edge.at[:, pl.ds(at, size)],
            edge_send.at[i], edge_recv.at[i], ctx_at(after),
        )

    for load in loads[:3]:
        load.wait()
    c_row, b_row, wide_cols, i, j = gates(logit_ref, g_ref)

    def col(h):
        return wide_cols[:, h : h + 1]

    def beta(h):
        return wide_cols[:, heads + h : heads + h + 1]

    for h in range(heads):
        ratio_ref[h] = ratios_of(col(h), c_row[h : h + 1, :], i, j)
    last_from = lax.rem(me + 1, n)
    own.wait()

    def convolve(i):
        at, size = parts[i]

        @pl.when(last_from != 0)
        def _():
            take_x(i, last_from)

        send_edge(i).start()
        for d in range(n - 1, 0, -1):

            @pl.when(last_from != d)
            def _():
                take_x(i, d)

        send_edge(i).wait_recv()
        span = slice(at, at + size)
        ext[0:EDGE, span] = jnp.where(c > 0, edge[:, span].astype(f32), 0.0)
        ext[EDGE : EDGE + rows, span] = x_in[:, span].astype(f32)
        conv = w_ref[KW - 1 : KW, span] * ext[EDGE : EDGE + rows, span]
        for tap in range(KW - 1):
            row = EDGE - (KW - 1) + tap
            conv = conv + w_ref[tap : tap + 1, span] * ext[row : row + rows, span]
        sig = 1.0 / (1.0 + jnp.exp(-conv))
        conv_ref[:, span] = conv
        sig_ref[:, span] = sig
        return conv * sig

    b = convolve(0)
    k = b * inv_norm(b)
    qk_ref[:, DK:] = k
    ks = split(k)
    gram = mm(ks, ks, 1, 1)
    lows = []
    for h in range(heads):
        rg = jnp.where(j < i, ratio_ref[h] * gram, 0.0)
        gram_ref[h] = rg
        lows.append(beta(h) * rg)
    diag = []
    for part in lows:
        diag += [part[:half, :half], part[half:, half:]]
    diag = invert_unit_lower(diag, half)
    for h in range(heads):
        one, two = split(diag[2 * h]), split(diag[2 * h + 1])
        corner = mm(split(mm(two, split(lows[h][half:, :half]))), one)
        solve_ref[h, :half, :half] = diag[2 * h]
        solve_ref[h, :half, half:] = jnp.zeros((half, half), f32)
        solve_ref[h, half:, :half] = -corner
        solve_ref[h, half:, half:] = diag[2 * h + 1]
    ii = lax.broadcasted_iota(jnp.int32, (DK, DK), 0)
    jj = lax.broadcasted_iota(jnp.int32, (DK, DK), 1)

    def tail_keys(h):
        return jnp.exp(col(h)[rows - 1 : rows, :] - col(h))

    for h in range(heads):
        weights = mm(split(solve_ref[h]), split((beta(h) * jnp.exp(col(h))) * k))
        weight_ref[h] = weights
        total_decay = jnp.exp(col(h)[rows - 1 : rows, :])
        a_mine[h] = jnp.where(ii == jj, total_decay, 0.0) - mm(
            split(weights), split(tail_keys(h) * k), 0, 0
        )
    swap_a = remote(a_mine.at[1 - k_at], a_sib, swap_send.at[0], swap_recv.at[0], sibling)
    swap_a.start()
    swap_a.wait_recv()
    mine, theirs = a_mine[k_at], a_sib[...]
    a1 = split(jnp.where(low, mine, theirs))
    a2 = split(jnp.where(low, theirs, mine))
    every[q_at] = mm(a1, a2)

    def a_copy(d):
        return remote(
            every.at[q_at], every.at[q_at], a_send.at[d], a_recv.at[q_at], chip(chip_off(d))
        )

    for d in far_first(chips):
        a_copy(d).start()

    a = convolve(1)
    q = a * (inv_norm(a) * DK**-0.5)
    qk_ref[:, :DK] = q
    qk = mm(split(q), ks, 1, 1)
    for load in loads[3:]:
        load.wait()
    for h in range(heads):
        score_ref[h] = ratio_ref[h] * qk
        score = split(score_ref[h])
        do = (do_ref[:, h * DV : (h + 1) * DV],)
        reach = jnp.exp(col(h)) * q - mm(score, split(weight_ref[h]))
        bc_mine[h, 1] = mm(do, split(reach), 0, 0)
        push_ref[h] = mm(score, do, 0, 0)
    values = convolve(2)
    for h in range(heads):
        base = mm(split(solve_ref[h]), split(beta(h) * values[:, h * DV : (h + 1) * DV]))
        base_ref[h] = base
        bc_mine[h, 0] = mm(split(base), split(tail_keys(h) * k), 0, 0)
    swap_bc = remote(bc_mine.at[1 - k_at], bc_sib, swap_send.at[1], swap_recv.at[1], sibling)
    swap_bc.start()
    swap_bc.wait_recv()
    mine, theirs = bc_mine[k_at], bc_sib[...]
    b1, c1 = jnp.where(low, mine[0], theirs[0]), jnp.where(low, mine[1], theirs[1])
    b2, c2 = jnp.where(low, theirs[0], mine[0]), jnp.where(low, theirs[1], mine[1])
    b12 = mm(split(b1), a2) + b2
    c12 = mm(split(c2), a1, 1, 1) + c1
    cut_out[:, :share, :] = b12.reshape(chips, share, DK)
    cut_out[:, share:, :] = c12.reshape(chips, share, DK)

    def cut_copy(d):
        to = chip_off(d)
        return remote(cut_out.at[to], cut_in.at[q_at], cut_send.at[d], cut_recv.at[q_at], chip(to))

    for d in far_first(chips):
        cut_copy(d).start()
    cut_in[q_at] = cut_out[q_at]
    start[...] = start[...].T
    end[...] = end[...].T
    my_rows = pl.ds(pl.multiple_of(q_at * share, share), share)
    s, d = start[my_rows, :], end[my_rows, :]
    here = set()

    def arrive(p):
        if p in here:
            return
        here.add(p)

        @pl.when(q_at != p)
        def _():
            remote(every.at[p], every.at[p], a_send.at[0], a_recv.at[p], chip(p)).wait_recv()
            remote(cut_out.at[p], cut_in.at[p], cut_send.at[0], cut_recv.at[p], chip(p)).wait_recv()

    def hand_out(p, value, out, into, send, recv):
        out[p] = value

        @pl.when(q_at != p)
        def _():
            remote(out.at[p], into.at[my_rows, :], send.at[p], recv.at[q_at], chip(p)).start()

        @pl.when(q_at == p)
        def _():
            into[my_rows, :] = value

    for t in range(chips):
        u = chips - 1 - t
        hand_out(t, s, s_out, s_in, s_send, s_recv)
        hand_out(u, d, d_out, d_in, d_send, d_recv)
        if t < chips - 1:
            arrive(t)
            arrive(u)
            s = mm(split(s), split(every[t])) + cut_in[t, :share, :]
            d = mm(split(d), split(every[u]), 1, 1) + cut_in[u, share:, :]

    def tile(p, out, into, send, recv):
        return remote(
            out.at[p], into.at[pl.ds(p * share, share), :], send.at[p], recv.at[p], chip(p)
        )

    for p in range(chips):

        @pl.when(q_at != p)
        def _():
            tile(p, s_out, s_in, s_send, s_recv).wait_recv()
            tile(p, d_out, d_in, d_send, d_recv).wait_recv()

    s, d = s_in[...], d_in[...]
    s2 = mm(split(s), a1) + b1
    d1 = mm(split(d), a2, 1, 1) + c2
    give[0] = jnp.where(low, s2, s)
    give[1] = jnp.where(low, d, d1)
    pass_on = remote(give, state_ref.at[k_at], swap_send.at[2], swap_recv.at[2], sibling)
    pass_on.start()
    state_ref[k_at, 0] = jnp.where(low, s, s2)
    state_ref[k_at, 1] = jnp.where(low, d1, d)
    pass_on.wait_recv()

    dext[0:EDGE, :] = jnp.zeros((EDGE, width), f32)
    dext[EDGE + rows :, :] = jnp.zeros((dext.shape[0] - EDGE - rows, width), f32)

    def silu_slope(span):
        s = sig_ref[:, span]
        return s * (1.0 + conv_ref[:, span] * (1.0 - s))

    spans = ((2 * DK, heads * DV), (0, 2 * DK))

    def spill_copy(i):
        at, size = spans[i]
        span = pl.ds(at, size)
        return remote(
            spill_ref.at[:, span], inbox.at[:, span],
            spill_send.at[i], spill_recv.at[i], ctx_at(before),
        )

    def send_back(i, d, source=None):
        at, size = spans[i]
        to = lax.rem(me + d, n)
        if source is None:
            source = own_ref.at[pl.ds(pl.multiple_of(to * slab, slab), slab), :]
        return remote(
            source.at[:, pl.ds(at, size)], out_hbm.at[:, cols(me, at, size)],
            back_send.at[i, d], back_recv.at[i, d], head_at(to),
        )

    def unconvolve(i):
        at, size = spans[i]
        span = slice(at, at + size)
        own = w_ref[KW - 1 : KW, span] * dext[EDGE : EDGE + rows, span]
        spill = w_ref[KW - 1 : KW, span] * dext[0:EDGE, span]
        for tap in range(KW - 1):
            back = KW - 1 - tap
            own = own + w_ref[tap : tap + 1, span] * dext[EDGE + back : EDGE + back + rows, span]
            spill = spill + w_ref[tap : tap + 1, span] * dext[back : back + EDGE, span]
        spill_ref[:, span] = spill
        spill_copy(i).start()
        own_ref[:, span] = own.astype(bf16)
        tail_ref[:, span] = own[rows - slab :, :]
        for d in far_first(n):

            @pl.when(lax.rem(me + d, n) != n - 1)
            def _():
                send_back(i, d).start()

    q, k = qk_ref[:, :DK], qk_ref[:, DK:]
    qs, ks = split(q), split(k)
    lower = j < i
    kept = []
    for h in range(heads):
        sts, dsts = split(state_ref[h, 0]), split(state_ref[h, 1])
        tail_k = tail_keys(h) * k
        update = base_ref[h] - mm(split(weight_ref[h]), sts, 1, 1)
        d_update = push_ref[h] + mm(split(tail_k), dsts, 1, 1)
        x = mm(split(solve_ref[h]), split(d_update), 0, 0)
        span = slice(2 * DK + h * DV, 2 * DK + (h + 1) * DV)
        dext[EDGE : EDGE + rows, span] = (beta(h) * x) * silu_slope(span)
        v = conv_ref[:, span] * sig_ref[:, span]
        kept.append((sts, dsts, tail_k, split(update), split(x), jnp.sum(x * v, axis=1, keepdims=True)))
    unconvolve(0)
    dq = None
    row_terms, col_terms = [], []
    for h in range(heads):
        sts, dsts, tail_k, us, xs, xv = kept[h]
        decays = jnp.exp(col(h))
        total_decay = jnp.exp(col(h)[rows - 1 : rows, :])
        ratios = ratio_ref[h]
        score = score_ref[h]
        do = (do_ref[:, h * DV : (h + 1) * DV],)
        d_score = mm(do, us, 1, 1)
        d_low = -mm(xs, us, 1, 1)
        y = -mm(xs, sts)
        d_tail = mm(us, dsts)
        rgd = gram_ref[h] * d_low
        part_q = decays * mm(do, sts)
        part_k = tail_keys(h) * d_tail + (beta(h) * decays) * y
        z = ratios * d_score
        d_gram = jnp.where(lower, beta(h) * (ratios * d_low), 0.0)
        if dq is None:
            dq, dk, zs, dgs = part_q, part_k, z, d_gram
        else:
            dq, dk, zs, dgs = dq + part_q, dk + part_k, zs + z, dgs + d_gram
        flow = jnp.where(lower, score * d_score, 0.0) + beta(h) * rgd
        yk = decays * jnp.sum(y * k, axis=1, keepdims=True)
        tk = jnp.sum(tail_k * d_tail, axis=1, keepdims=True)
        d_beta = xv + yk + jnp.sum(rgd, axis=1, keepdims=True)
        d_cum = (
            jnp.sum(flow, axis=1, keepdims=True)
            + jnp.sum(q * part_q, axis=1, keepdims=True)
            + beta(h) * yk
            - tk
        )
        ends = total_decay * jnp.sum(
            state_ref[h, 0] * state_ref[h, 1], keepdims=True
        ) + jnp.sum(tk, keepdims=True)
        at_end = lax.broadcasted_iota(jnp.int32, (rows, 1), 0) == rows - 1
        col_terms.append((d_cum + jnp.where(at_end, ends, 0.0), d_beta))
        row_terms.append(jnp.sum(flow, axis=0, keepdims=True))
    zs, dgs = split(zs), split(dgs)
    dq = dq + mm(zs, ks)
    dk = dk + mm(zs, qs, 0, 0) + mm(dgs, ks) + mm(dgs, ks, 0, 0)
    for at, d, factor in ((0, dq, DK**-0.5), (DK, dk, 1.0)):
        span = slice(at, at + DK)
        value = conv_ref[:, span] * sig_ref[:, span]
        inv = inv_norm(value)
        inner = jnp.sum(value * d, axis=1, keepdims=True)
        d_act = (inv * factor) * (d - value * (inv * inv * inner))
        dext[EDGE : EDGE + rows, span] = d_act * silu_slope(span)
    unconvolve(1)
    d_conv = dext[EDGE : EDGE + rows, :]
    for tap in range(KW):
        row = EDGE - (KW - 1) + tap
        gw_ref[tap : tap + 1, :] = jnp.sum(d_conv * ext[row : row + rows, :], axis=0, keepdims=True)
    swap_gw = remote(gw_ref, gw_sib, swap_send.at[3], swap_recv.at[3], sibling)
    swap_gw.start()

    for i_part in range(2):
        spill_copy(i_part).wait_recv()
    last_ref[...] = tail_ref[...].astype(bf16)
    more = jnp.where(c < nc - 1, inbox[...], 0.0)
    last_ref[slab - EDGE :, :] = (tail_ref[slab - EDGE :, :] + more).astype(bf16)
    to_last = lax.rem(2 * n - 1 - me, n)
    mine_out = out_hbm.at[:, cols(me)]
    own_back = pltpu.make_async_copy(
        own_ref.at[pl.ds(pl.multiple_of(me * slab, slab), slab), :], mine_out, own_sem
    )
    last_back = pltpu.make_async_copy(last_ref, mine_out, own_sem)

    @pl.when(me != n - 1)
    def _():
        for i_part in range(2):
            send_back(i_part, to_last, last_ref).start()
        own_back.start()

    @pl.when(me == n - 1)
    def _():
        last_back.start()

    swap_gw.wait_recv()
    gw_all[q_at] = jnp.where(low, gw_ref[...], gw_sib[...]) + jnp.where(low, gw_sib[...], gw_ref[...])

    def gw_copy(d):
        return remote(
            gw_all.at[q_at], gw_all.at[q_at], gw_send.at[d], gw_recv.at[q_at], chip(chip_off(d))
        )

    for d in far_first(chips):
        gw_copy(d).start()
    lanes = lax.broadcasted_iota(jnp.int32, (rows, 8), 1)
    packed = jnp.zeros((rows, 8), f32)
    for h in range(heads):
        packed = jnp.where(lanes == h, col_terms[h][0], packed)
        packed = jnp.where(lanes == heads + h, col_terms[h][1], packed)
    packed = packed.T
    glogit_ref[...] = packed[heads : 2 * heads] * b_row * (1.0 - b_row)
    d_cum = packed[:heads] - jnp.concatenate(row_terms, axis=0)
    onward = jnp.where(i >= j, 1.0, 0.0).astype(bf16)
    d1 = d_cum.astype(bf16)
    rest = d_cum - d1.astype(f32)
    d2 = rest.astype(bf16)
    d3 = (rest - d2.astype(f32)).astype(bf16)
    gdecay_ref[...] = (dot(d3, onward, 1, 0) + dot(d2, onward, 1, 0)) + dot(d1, onward, 1, 0)
    stores = [
        pltpu.make_async_copy(glogit_ref, glogit_hbm, store_sem.at[0]),
        pltpu.make_async_copy(gdecay_ref, gdecay_hbm, store_sem.at[1]),
        pltpu.make_async_copy(total_ref, total_hbm, store_sem.at[2]),
    ]
    stores[0].start()
    stores[1].start()
    for d in range(1, chips):
        source = chip_off(d)
        remote(
            gw_all.at[q_at], gw_all.at[source], gw_send.at[d], gw_recv.at[source], chip(source)
        ).wait_recv()
    total = gw_all[0]
    for p in range(1, chips):
        total = total + gw_all[p]
    total_ref[...] = total
    stores[2].start()

    for i_part in range(3):
        for d in range(1, n):
            send_x(i_part, d).wait_send()
        send_edge(i_part).wait_send()
    for swap in (swap_a, swap_bc, pass_on, swap_gw):
        swap.wait_send()
    for d in range(1, chips):
        a_copy(d).wait_send()
        cut_copy(d).wait_send()
        gw_copy(d).wait_send()
    for p in range(chips):

        @pl.when(q_at != p)
        def _():
            tile(p, s_out, s_in, s_send, s_recv).wait_send()
            tile(p, d_out, d_in, d_send, d_recv).wait_send()

    for i_part in range(2):
        at, size = spans[i_part]
        spill_copy(i_part).wait_send()
        for d in range(1, n):
            source = lax.rem(me + n - d, n)
            send_back(i_part, d, last_ref).wait_send()
            remote(
                last_ref.at[:, pl.ds(at, size)], out_hbm.at[:, cols(source, at, size)],
                back_send.at[i_part, d], back_recv.at[i_part, d], head_at(source),
            ).wait_recv()
    last_back.wait()
    for store in stores:
        store.wait()


def on_device(mixed_in, conv_weight, logits, decay_log, initial_state, final_state_grad, grad_out):
    n, nc = lax.axis_size("head"), lax.axis_size("ctx")
    heads, rows = decay_log.shape
    slab = mixed_in.shape[0]
    width = mixed_in.shape[1] // n
    chips = nc // 2
    share = DV // chips
    sems = pltpu.SemaphoreType.DMA
    vm = pltpu.VMEM
    anywhere = pl.BlockSpec(memory_space=pltpu.HBM)
    square = vm((heads, rows, rows), f32)
    tall = vm((heads, rows, DK), f32)
    state = vm((DV, DK), f32)
    return pl.pallas_call(
        functools.partial(layer_kernel, n, nc),
        out_shape=(
            shape_of(*mixed_in.shape, dtype=bf16),
            shape_of(*conv_weight.shape),
            shape_of(heads, rows),
            shape_of(heads, rows),
        ),
        in_specs=[anywhere] * 7,
        out_specs=(anywhere,) * 4,
        scratch_shapes=[
            vm((KW, width), f32), vm((heads, rows), f32), vm((heads, rows), f32),
            vm((rows, heads * DV), bf16), state, state,
            vm((rows, width), bf16), vm((EDGE, width), bf16),
            vm((EDGE + rows, width), f32), vm((2 * EDGE + rows, width), f32),
            vm((rows, width), f32), vm((rows, width), f32), vm((rows, 2 * DK), f32),
            square, square, square, square, tall, tall, tall,
            vm((heads, DK, DK), f32), vm((heads, 2, DV, DK), f32), state, vm((2, DV, DK), f32),
            vm((chips, DK, DK), f32),
            vm((chips, 2 * share, DK), f32), vm((chips, 2 * share, DK), f32),
            vm((chips, share, DK), f32), vm((chips, share, DK), f32), state, state,
            vm((2, DV, DK), f32), vm((heads, 2, DV, DK), f32),
            vm((rows, width), bf16), vm((slab, width), f32), vm((EDGE, width), f32),
            vm((EDGE, width), f32), vm((slab, width), bf16),
            vm((KW, width), f32), vm((KW, width), f32), vm((chips, KW, width), f32),
            vm((KW, width), f32), vm((heads, rows), f32), vm((heads, rows), f32),
            sems((6,)), sems((3,)), sems,
            sems((3, n)), sems((3, n)), sems((3,)), sems((3,)), sems((4,)), sems((4,)),
            sems((chips,)), sems((chips,)), sems((chips,)), sems((chips,)),
            sems((chips,)), sems((chips,)), sems((chips,)), sems((chips,)),
            sems((2,)), sems((2,)), sems((2, n)), sems((2, n)), sems((chips,)), sems((chips,)),
        ],
        compiler_params=pltpu.CompilerParams(
            collective_id=1, has_side_effects=True, vmem_limit_bytes=63 << 20
        ),
        name="layer",
    )(mixed_in, conv_weight, logits, decay_log, grad_out, initial_state, final_state_grad)


def solution(mesh):
    in_specs = (
        P(("ctx", "head"), None),
        P(None, "head"),
        P("head", "ctx"),
        P("head", "ctx"),
        P("head", None, None),
        P("head", None, None),
        P("ctx", "head"),
    )
    out_specs = (P(("ctx", "head"), None), P(None, "head"), P("head", "ctx"), P("head", "ctx"))
    return jax.shard_map(
        on_device, mesh=mesh, in_specs=in_specs, out_specs=out_specs, check_vma=False
    )
```

time: 208 us -> 87.1 us (0.42); the launches traced: 205 us -> 86.9 us
  blocking collectives: 90.9 us -> 0 us
  starting transfers between devices: 86.6 us -> 0 us
  Pallas kernels: 9.93 us -> 82.7 us
  matrix products: 6.75 us -> 0 us
  waiting for transfers between devices: 5.38 us -> 0 us
    ppermute x22 -> x0, starting transfers between devices: 81.1 us -> none  [from_behind(): return lax.ppermute(value, axis, pairs)]
    pallas_call x2 -> x1, Pallas kernels: 9.93 us -> 82.7 us  [on_device(): pl.pallas_call(functools.partial(layer_kernel, n, nc), out_shape=(shape_o...]
    psum x1 -> x0, blocking collectives: 62 us -> none  [on_device(): return (returned, lax.psum(gw, 'ctx'), glogit, gdecay)]
    all_to_all x1 -> x0, blocking collectives: 28.8 us -> none  [on_device(): lax.all_to_all(mixed_in, 'head', split_axis=1, concat_axis=0, tiled=True)]
    dot_general x20 -> x0, matrix products: 6.75 us -> none  [the longest x8 3.16 us: sweep(): m = jnp.where(has, ein('hki,hij->hkj', mo, m), m)]
    all_to_all x1 -> x0, starting transfers between devices: 5.51 us -> none  [on_device(): lax.all_to_all(own, 'head', split_axis=0, concat_axis=1, tiled=True)]
    ppermute x22 -> x0, waiting for transfers between devices: 5.37 us -> none  [from_behind(): return lax.ppermute(value, axis, pairs)]
  transfers between devices with their start and end apart: 23 -> 0, of which waited for: 2 -> 0; matrix products, arithmetic and copies ran while one was open for 4% -> 0% of each run, Pallas kernels for 0% -> 0%
where the time goes in v3:
time: 87.1 us; the launch traced here: 86.9 us
  Pallas kernels  82.7 us (95%)
  local copies, waits for them, and re-layouts  3.59 us (4%)
    pallas_call x1, Pallas kernels, on_device(): pl.pallas_call(functools.partial(layer_kernel, n, nc), out_shape=(shape_o...  82.7 us
    unnamed x10, local copies, waits for them, and re-layouts  3.59 us

profile of v3, /device:TPU:1, one launch (start us, length us, event | category | flops | bytes accessed | tf_op | source)
XLA Modules:
  0.0 86.9 jit_solution(4554062664060729205)
XLA Ops:
  0.6 82.7 %layer.1 = (bf16[16,8192]{1,0:T(8,128)(2,1)}, f32[4,512]{1,0:T(4,128)}, f32[2,256]{1,0:T(2,128)}, f32[2,256]{1,0:T(2,128)}) custom-call(bf16[16,8192]{1,0:T(8,128)(2,1)} %x_hbm.1, f32[4,512]{1,0:T(4,128)} %w_hbm.1, f32[2,256]{1,0:T(2,128)} %logit_hbm.1, f32[2,256]{1,0:T(2,128)} %g_hbm.1, bf16[256,256]{1,0:T(8,128)(2,1)} %do_hbm.1, f32[2,128,128]{2,1,0:T(8,128)} %first_hbm.1, ...), custom_call_target="tpu_custom_call" | custom-call | tf_op jit(solution)/shard_map/layer/pallas_call | solution.py:626
  83.3 0.0 copy-start
  83.3 1.7 %copy.15 = bf16[16,8192]{1,0:T(8,128)(2,1)} copy(bf16[16,8192]{1,0:T(8,128)(2,1)} %get-tuple-element.8) | data formatting | bytes 524288
  85.0 0.0 copy-done
  85.0 0.0 copy-start.2
  85.0 0.6 copy.16
  85.6 0.1 copy-done.2
  85.7 0.0 copy-start.1
  85.7 0.6 copy.17
  86.3 0.1 copy-done.1
  86.4 0.6 copy.18
Async XLA Ops:
  83.3 1.7 %copy-start = (f32[4,512]{1,0:T(4,128)S(1)}, f32[4,512]{1,0:T(4,128)}, u32[]{:S(2)}) copy-start(f32[4,512]{1,0:T(4,128)} %get-tuple-element.9) | copy-start | bytes 24580
  85.0 0.7 copy-start.2
  85.7 0.7 copy-start.1

commit v4 on v3

--- a/solution.py
+++ b/solution.py
@@ -116,36 +116,67 @@
 
 
 def layer_kernel(
-    n, nc, x_hbm, w_hbm, logit_hbm, g_hbm, do_hbm, first_hbm, final_hbm,
+    n, nc, row_len, x_hbm, w_hbm, logit_hbm, g_hbm, do_hbm, first_hbm, final_hbm,
     out_hbm, total_hbm, glogit_hbm, gdecay_hbm,
     w_ref, logit_ref, g_ref, do_ref, start, end,
     x_in, edge, ext, dext, conv_ref, sig_ref, qk_ref,
     ratio_ref, gram_ref, score_ref, solve_ref, base_ref, weight_ref, push_ref,
-    a_mine, bc_mine, a_sib, bc_sib, every, cut_out, cut_in,
-    s_out, d_out, s_in, d_in, give, state_ref,
-    own_ref, tail_ref, spill_ref, inbox, last_ref,
-    gw_ref, gw_sib, gw_all, total_ref, glogit_ref, gdecay_ref,
+    a_mine, bc_mine, a_sib, bc_sib, row_a, col_a, cut_out, cut_in, row_bc, tile_out, tile_in,
+    state_ref, own_ref, tail_ref, spill_ref, inbox, last_ref,
+    gw_ref, gw_sib, gw_row, gw_col, total_ref, glogit_ref, gdecay_ref,
     load_sem, store_sem, own_sem, x_send, x_recv, edge_send, edge_recv, swap_send, swap_recv,
-    a_send, a_recv, cut_send, cut_recv, s_send, s_recv, d_send, d_recv,
-    spill_send, spill_recv, back_send, back_recv, gw_send, gw_recv,
+    row_send, row_recv, col_send, col_recv, tile_send, tile_recv,
+    spill_send, spill_recv, back_send, back_recv,
 ):
     me, c = lax.axis_index("head"), lax.axis_index("ctx")
     heads, rows = g_ref.shape
     slab, width = x_hbm.shape[0], x_in.shape[1]
     half = rows // 2
-    chips = nc // 2
-    share = DV // chips
-    q_at, k_at = lax.div(c, 2), lax.rem(c, 2)
+    col_len = nc // (2 * row_len)
+    share = DV // row_len
+    k_at = lax.rem(c, 2)
+    y_at = lax.rem(lax.div(c, 2), row_len)
+    x_at = lax.div(c, 2 * row_len)
     low = k_at == 0
     after, before = lax.rem(c + 1, nc), lax.rem(c + nc - 1, nc)
     sibling = ctx_at(c + 1 - 2 * k_at)
     other = ctx_at(lax.rem(c + nc - 1 + 2 * k_at, nc))
 
-    def chip(p):
-        return ctx_at(2 * p + k_at)
-
-    def chip_off(d):
-        return lax.rem(q_at + d, chips)
+    def in_row(y, parity):
+        return ctx_at((x_at * row_len + y) * 2 + parity)
+
+    def in_col(x):
+        return ctx_at((x * row_len + y_at) * 2 + k_at)
+
+    def row_off(d):
+        return lax.rem(y_at + d, row_len)
+
+    def col_off(d):
+        return lax.rem(x_at + d, col_len)
+
+    def to_row(kind, d, source, target):
+        return remote(
+            source, target, row_send.at[kind, d], row_recv.at[kind, y_at], in_row(row_off(d), k_at)
+        )
+
+    def from_row(kind, d, buffer):
+        y = row_off(d)
+        remote(
+            buffer.at[y], buffer.at[y], row_send.at[kind, d], row_recv.at[kind, y], in_row(y, k_at)
+        ).wait_recv()
+
+    def to_col(kind, d, source, target):
+        return remote(
+            source, target, col_send.at[kind, d], col_recv.at[kind, x_at], in_col(col_off(d))
+        )
+
+    def from_col(kind, d, buffer):
+        x = col_off(d)
+        remote(
+            buffer.at[x], buffer.at[x], col_send.at[kind, d], col_recv.at[kind, x], in_col(x)
+        ).wait_recv()
+
+    row_steps, col_steps = range(1, row_len), range(1, col_len)
 
     loads = [
         pltpu.make_async_copy(source, target, load_sem.at[i])
@@ -173,7 +204,9 @@
     own.start()
     greet(
         [head_at(lax.rem(me + d, n)) for d in far_first(n)]
-        + [chip(chip_off(d)) for d in far_first(chips)]
+        + [in_row(row_off(d), k_at) for d in row_steps]
+        + [in_row(row_off(d), 1 - k_at) for d in row_steps]
+        + [in_col(col_off(d)) for d in col_steps]
         + [sibling, other]
     )
 
@@ -285,21 +318,19 @@
         a_mine[h] = jnp.where(ii == jj, total_decay, 0.0) - mm(
             split(weights), split(tail_keys(h) * k), 0, 0
         )
-    swap_a = remote(a_mine.at[1 - k_at], a_sib, swap_send.at[0], swap_recv.at[0], sibling)
+    swap_a = remote(a_mine, a_sib, swap_send.at[0], swap_recv.at[0], sibling)
     swap_a.start()
     swap_a.wait_recv()
-    mine, theirs = a_mine[k_at], a_sib[...]
+    mine, theirs = a_mine[k_at], a_sib[k_at]
     a1 = split(jnp.where(low, mine, theirs))
     a2 = split(jnp.where(low, theirs, mine))
-    every[q_at] = mm(a1, a2)
-
-    def a_copy(d):
-        return remote(
-            every.at[q_at], every.at[q_at], a_send.at[d], a_recv.at[q_at], chip(chip_off(d))
-        )
-
-    for d in far_first(chips):
-        a_copy(d).start()
+    row_a[y_at] = mm(a1, a2)
+
+    def row_a_copy(d):
+        return to_row(0, d, row_a.at[y_at], row_a.at[y_at])
+
+    for d in row_steps:
+        row_a_copy(d).start()
 
     a = convolve(1)
     q = a * (inv_norm(a) * DK**-0.5)
@@ -319,83 +350,102 @@
         base = mm(split(solve_ref[h]), split(beta(h) * values[:, h * DV : (h + 1) * DV]))
         base_ref[h] = base
         bc_mine[h, 0] = mm(split(base), split(tail_keys(h) * k), 0, 0)
-    swap_bc = remote(bc_mine.at[1 - k_at], bc_sib, swap_send.at[1], swap_recv.at[1], sibling)
+    swap_bc = remote(bc_mine, bc_sib, swap_send.at[1], swap_recv.at[1], sibling)
     swap_bc.start()
+    for d in row_steps:
+        from_row(0, d, row_a)
+    steps = [split(row_a[y]) for y in range(row_len)]
+    ahead = {row_len - 2: steps[row_len - 1]}
+    for y in range(row_len - 3, -1, -1):
+        ahead[y] = split(mm(steps[y + 1], ahead[y + 1]))
+    behind = {1: steps[0]}
+    for y in range(2, row_len):
+        behind[y] = split(mm(behind[y - 1], steps[y - 1]))
+    col_a[x_at] = mm(behind[row_len // 2], ahead[row_len // 2 - 1])
+
+    def col_a_copy(d):
+        return to_col(0, d, col_a.at[x_at], col_a.at[x_at])
+
+    for d in col_steps:
+        col_a_copy(d).start()
     swap_bc.wait_recv()
-    mine, theirs = bc_mine[k_at], bc_sib[...]
+    mine, theirs = bc_mine[k_at], bc_sib[k_at]
     b1, c1 = jnp.where(low, mine[0], theirs[0]), jnp.where(low, mine[1], theirs[1])
     b2, c2 = jnp.where(low, theirs[0], mine[0]), jnp.where(low, theirs[1], mine[1])
     b12 = mm(split(b1), a2) + b2
     c12 = mm(split(c2), a1, 1, 1) + c1
-    cut_out[:, :share, :] = b12.reshape(chips, share, DK)
-    cut_out[:, share:, :] = c12.reshape(chips, share, DK)
+    cut_out[:, :share, :] = b12.reshape(row_len, share, DK)
+    cut_out[:, share:, :] = c12.reshape(row_len, share, DK)
 
     def cut_copy(d):
-        to = chip_off(d)
-        return remote(cut_out.at[to], cut_in.at[q_at], cut_send.at[d], cut_recv.at[q_at], chip(to))
-
-    for d in far_first(chips):
+        return to_row(1, d, cut_out.at[row_off(d)], cut_in.at[y_at])
+
+    for d in row_steps:
         cut_copy(d).start()
-    cut_in[q_at] = cut_out[q_at]
+    cut_in[y_at] = cut_out[y_at]
     start[...] = start[...].T
     end[...] = end[...].T
-    my_rows = pl.ds(pl.multiple_of(q_at * share, share), share)
-    s, d = start[my_rows, :], end[my_rows, :]
-    here = set()
-
-    def arrive(p):
-        if p in here:
-            return
-        here.add(p)
-
-        @pl.when(q_at != p)
-        def _():
-            remote(every.at[p], every.at[p], a_send.at[0], a_recv.at[p], chip(p)).wait_recv()
-            remote(cut_out.at[p], cut_in.at[p], cut_send.at[0], cut_recv.at[p], chip(p)).wait_recv()
-
-    def hand_out(p, value, out, into, send, recv):
-        out[p] = value
-
-        @pl.when(q_at != p)
-        def _():
-            remote(out.at[p], into.at[my_rows, :], send.at[p], recv.at[q_at], chip(p)).start()
-
-        @pl.when(q_at == p)
-        def _():
-            into[my_rows, :] = value
-
-    for t in range(chips):
-        u = chips - 1 - t
-        hand_out(t, s, s_out, s_in, s_send, s_recv)
-        hand_out(u, d, d_out, d_in, d_send, d_recv)
-        if t < chips - 1:
-            arrive(t)
-            arrive(u)
-            s = mm(split(s), split(every[t])) + cut_in[t, :share, :]
-            d = mm(split(d), split(every[u]), 1, 1) + cut_in[u, share:, :]
-
-    def tile(p, out, into, send, recv):
+    for d in row_steps:
+        from_row(1, d, cut_in)
+    gained = {1: cut_in[0, :share, :]}
+    owed = {row_len - 2: cut_in[row_len - 1, share:, :]}
+    for t in range(1, row_len):
+        u = row_len - 1 - t
+        gained[t + 1] = mm(split(gained[t]), steps[t]) + cut_in[t, :share, :]
+        owed[u - 1] = mm(split(owed[u]), steps[u], 1, 1) + cut_in[u, share:, :]
+    row_bc[x_at, :share, :] = gained[row_len]
+    row_bc[x_at, share:, :] = owed[-1]
+
+    def row_bc_copy(d):
+        return to_col(1, d, row_bc.at[x_at], row_bc.at[x_at])
+
+    for d in col_steps:
+        row_bc_copy(d).start()
+    my_rows = pl.ds(pl.multiple_of(y_at * share, share), share)
+    s, d_state = start[my_rows, :], end[my_rows, :]
+    for d in col_steps:
+        from_col(0, d, col_a)
+    leaps = [split(col_a[x]) for x in range(col_len)]
+    for d in col_steps:
+        from_col(1, d, row_bc)
+    for t in range(col_len - 1):
+        u = col_len - 1 - t
+        s = jnp.where(t < x_at, mm(split(s), leaps[t]) + row_bc[t, :share, :], s)
+        back = mm(split(d_state), leaps[u], 1, 1) + row_bc[u, share:, :]
+        d_state = jnp.where(u > x_at, back, d_state)
+    ss, ds = split(s), split(d_state)
+    for y in range(row_len):
+        tile_out[y, :share, :] = mm(ss, behind[y]) + gained[y] if y else s
+        tile_out[y, share:, :] = mm(ds, ahead[y], 1, 1) + owed[y] if y < row_len - 1 else d_state
+
+    def tile_copy(d, flip):
+        y = row_off(d)
+        parity = k_at + flip - 2 * k_at * flip
         return remote(
-            out.at[p], into.at[pl.ds(p * share, share), :], send.at[p], recv.at[p], chip(p)
-        )
-
-    for p in range(chips):
-
-        @pl.when(q_at != p)
-        def _():
-            tile(p, s_out, s_in, s_send, s_recv).wait_recv()
-            tile(p, d_out, d_in, d_send, d_recv).wait_recv()
-
-    s, d = s_in[...], d_in[...]
-    s2 = mm(split(s), a1) + b1
-    d1 = mm(split(d), a2, 1, 1) + c2
-    give[0] = jnp.where(low, s2, s)
-    give[1] = jnp.where(low, d, d1)
-    pass_on = remote(give, state_ref.at[k_at], swap_send.at[2], swap_recv.at[2], sibling)
-    pass_on.start()
-    state_ref[k_at, 0] = jnp.where(low, s, s2)
-    state_ref[k_at, 1] = jnp.where(low, d1, d)
-    pass_on.wait_recv()
+            tile_out.at[y], tile_in.at[k_at, y_at],
+            tile_send.at[flip, d], tile_recv.at[k_at, y_at], in_row(y, parity),
+        )
+
+    def tile_wait(d, flip):
+        y = row_off(d)
+        parity = k_at + flip - 2 * k_at * flip
+        remote(
+            tile_out.at[y], tile_in.at[parity, y],
+            tile_send.at[flip, d], tile_recv.at[parity, y], in_row(y, parity),
+        ).wait_recv()
+
+    tile_steps = [(d, flip) for d in row_steps for flip in (0, 1)] + [(0, 1)]
+    for d, flip in tile_steps:
+        tile_copy(d, flip).start()
+    tile_in[k_at, y_at] = tile_out[y_at]
+    for d, flip in tile_steps:
+        tile_wait(d, flip)
+    for h in range(heads):
+        s = tile_in[h, :, :share, :].reshape(DV, DK)
+        d_state = tile_in[h, :, share:, :].reshape(DV, DK)
+        theirs = split(a_sib[h])
+        state_ref[h, 0] = jnp.where(low, s, mm(split(s), theirs) + bc_sib[h, 0])
+        state_ref[h, 1] = jnp.where(low, mm(split(d_state), theirs, 1, 1) + bc_sib[h, 1], d_state)
 
     dext[0:EDGE, :] = jnp.zeros((EDGE, width), f32)
     dext[EDGE + rows :, :] = jnp.zeros((dext.shape[0] - EDGE - rows, width), f32)
@@ -511,7 +561,7 @@
     for tap in range(KW):
         row = EDGE - (KW - 1) + tap
         gw_ref[tap : tap + 1, :] = jnp.sum(d_conv * ext[row : row + rows, :], axis=0, keepdims=True)
-    swap_gw = remote(gw_ref, gw_sib, swap_send.at[3], swap_recv.at[3], sibling)
+    swap_gw = remote(gw_ref, gw_sib, swap_send.at[2], swap_recv.at[2], sibling)
     swap_gw.start()
 
     for i_part in range(2):
@@ -537,15 +587,16 @@
         last_back.start()
 
     swap_gw.wait_recv()
-    gw_all[q_at] = jnp.where(low, gw_ref[...], gw_sib[...]) + jnp.where(low, gw_sib[...], gw_ref[...])
-
-    def gw_copy(d):
-        return remote(
-            gw_all.at[q_at], gw_all.at[q_at], gw_send.at[d], gw_recv.at[q_at], chip(chip_off(d))
-        )
-
-    for d in far_first(chips):
-        gw_copy(d).start()
+    gw_row[y_at] = jnp.where(low, gw_ref[...], gw_sib[...]) + jnp.where(low, gw_sib[...], gw_ref[...])
+
+    def gw_row_copy(d):
+        return to_row(2, d, gw_row.at[y_at], gw_row.at[y_at])
+
+    def gw_col_copy(d):
+        return to_col(2, d, gw_col.at[x_at], gw_col.at[x_at])
+
+    for d in row_steps:
+        gw_row_copy(d).start()
     lanes = lax.broadcasted_iota(jnp.int32, (rows, 8), 1)
     packed = jnp.zeros((rows, 8), f32)
     for h in range(heads):
@@ -567,14 +618,19 @@
     ]
     stores[0].start()
     stores[1].start()
-    for d in range(1, chips):
-        source = chip_off(d)
-        remote(
-            gw_all.at[q_at], gw_all.at[source], gw_send.at[d], gw_recv.at[source], chip(source)
-        ).wait_recv()
-    total = gw_all[0]
-    for p in range(1, chips):
-        total = total + gw_all[p]
+    for d in row_steps:
+        from_row(2, d, gw_row)
+    total = gw_row[0]
+    for y in range(1, row_len):
+        total = total + gw_row[y]
+    gw_col[x_at] = total
+    for d in col_steps:
+        gw_col_copy(d).start()
+    for d in col_steps:
+        from_col(2, d, gw_col)
+    total = gw_col[0]
+    for x in range(1, col_len):
+        total = total + gw_col[x]
     total_ref[...] = total
     stores[2].start()
 
@@ -582,18 +638,18 @@
         for d in range(1, n):
             send_x(i_part, d).wait_send()
         send_edge(i_part).wait_send()
-    for swap in (swap_a, swap_bc, pass_on, swap_gw):
+    for swap in (swap_a, swap_bc, swap_gw):
         swap.wait_send()
-    for d in range(1, chips):
-        a_copy(d).wait_send()
+    for d in row_steps:
+        row_a_copy(d).wait_send()
         cut_copy(d).wait_send()
-        gw_copy(d).wait_send()
-    for p in range(chips):
-
-        @pl.when(q_at != p)
-        def _():
-            tile(p, s_out, s_in, s_send, s_recv).wait_send()
-            tile(p, d_out, d_in, d_send, d_recv).wait_send()
+        gw_row_copy(d).wait_send()
+    for d in col_steps:
+        col_a_copy(d).wait_send()
+        row_bc_copy(d).wait_send()
+        gw_col_copy(d).wait_send()
+    for d, flip in tile_steps:
+        tile_copy(d, flip).wait_send()
 
     for i_part in range(2):
         at, size = spans[i_part]
@@ -610,21 +666,27 @@
         store.wait()
 
 
+def settle_kernel(*refs):
+    for source, target in zip(refs[:4], refs[4:]):
+        target[...] = source[...]
+
+
 def on_device(mixed_in, conv_weight, logits, decay_log, initial_state, final_state_grad, grad_out):
     n, nc = lax.axis_size("head"), lax.axis_size("ctx")
     heads, rows = decay_log.shape
     slab = mixed_in.shape[0]
     width = mixed_in.shape[1] // n
-    chips = nc // 2
-    share = DV // chips
+    row_len = 4
+    col_len = nc // (2 * row_len)
+    share = DV // row_len
     sems = pltpu.SemaphoreType.DMA
     vm = pltpu.VMEM
     anywhere = pl.BlockSpec(memory_space=pltpu.HBM)
     square = vm((heads, rows, rows), f32)
     tall = vm((heads, rows, DK), f32)
     state = vm((DV, DK), f32)
-    return pl.pallas_call(
-        functools.partial(layer_kernel, n, nc),
+    results = pl.pallas_call(
+        functools.partial(layer_kernel, n, nc, row_len),
         out_shape=(
             shape_of(*mixed_in.shape, dtype=bf16),
             shape_of(*conv_weight.shape),
@@ -640,26 +702,33 @@
             vm((EDGE + rows, width), f32), vm((2 * EDGE + rows, width), f32),
             vm((rows, width), f32), vm((rows, width), f32), vm((rows, 2 * DK), f32),
             square, square, square, square, tall, tall, tall,
-            vm((heads, DK, DK), f32), vm((heads, 2, DV, DK), f32), state, vm((2, DV, DK), f32),
-            vm((chips, DK, DK), f32),
-            vm((chips, 2 * share, DK), f32), vm((chips, 2 * share, DK), f32),
-            vm((chips, share, DK), f32), vm((chips, share, DK), f32), state, state,
-            vm((2, DV, DK), f32), vm((heads, 2, DV, DK), f32),
+            vm((heads, DK, DK), f32), vm((heads, 2, DV, DK), f32),
+            vm((heads, DK, DK), f32), vm((heads, 2, DV, DK), f32),
+            vm((row_len, DK, DK), f32), vm((col_len, DK, DK), f32),
+            vm((row_len, 2 * share, DK), f32), vm((row_len, 2 * share, DK), f32),
+            vm((col_len, 2 * share, DK), f32), vm((row_len, 2 * share, DK), f32),
+            vm((2, row_len, 2 * share, DK), f32), vm((heads, 2, DV, DK), f32),
             vm((rows, width), bf16), vm((slab, width), f32), vm((EDGE, width), f32),
             vm((EDGE, width), f32), vm((slab, width), bf16),
-            vm((KW, width), f32), vm((KW, width), f32), vm((chips, KW, width), f32),
+            vm((KW, width), f32), vm((KW, width), f32),
+            vm((row_len, KW, width), f32), vm((col_len, KW, width), f32),
             vm((KW, width), f32), vm((heads, rows), f32), vm((heads, rows), f32),
             sems((6,)), sems((3,)), sems,
-            sems((3, n)), sems((3, n)), sems((3,)), sems((3,)), sems((4,)), sems((4,)),
-            sems((chips,)), sems((chips,)), sems((chips,)), sems((chips,)),
-            sems((chips,)), sems((chips,)), sems((chips,)), sems((chips,)),
-            sems((2,)), sems((2,)), sems((2, n)), sems((2, n)), sems((chips,)), sems((chips,)),
+            sems((3, n)), sems((3, n)), sems((3,)), sems((3,)), sems((3,)), sems((3,)),
+            sems((3, row_len)), sems((3, row_len)), sems((3, col_len)), sems((3, col_len)),
+            sems((2, row_len)), sems((2, row_len)),
+            sems((2,)), sems((2,)), sems((2, n)), sems((2, n)),
         ],
         compiler_params=pltpu.CompilerParams(
             collective_id=1, has_side_effects=True, vmem_limit_bytes=63 << 20
         ),
         name="layer",
     )(mixed_in, conv_weight, logits, decay_log, grad_out, initial_state, final_state_grad)
+    return pl.pallas_call(
+        settle_kernel,
+        out_shape=tuple(shape_of(*part.shape, dtype=part.dtype) for part in results),
+        name="settle",
+    )(*results)
 
 
 def solution(mesh):

time: 87.1 us -> 72.7 us (0.83)
  Pallas kernels: 82.7 us -> 71.9 us
  local copies, waits for them, and re-layouts: 3.59 us -> 0 us
    pallas_call x1 -> x2, Pallas kernels: 82.7 us -> 71.9 us  [the longest x1 70.2 us: on_device(): pl.pallas_call(functools.partial(layer_kernel, n, nc, row_len), out_shape...]
    unnamed x10 -> x0, local copies, waits for them, and re-layouts: 3.59 us -> none
where the time goes in v4:
time: 72.7 us; the launch traced here: 72.6 us
  Pallas kernels  71.9 us (99%)
    pallas_call x1, Pallas kernels, on_device(): pl.pallas_call(functools.partial(layer_kernel, n, nc, row_len), out_shape...  70.2 us
    pallas_call x1, Pallas kernels, on_device(): pl.pallas_call(settle_kernel, out_shape=tuple((shape_of(*part.shape, dtyp...  1.7 us

profile of v4, /device:TPU:1, one launch (start us, length us, event | category | flops | bytes accessed | tf_op | source)
XLA Modules:
  0.0 72.6 jit_solution(17802024814664108215)
XLA Ops:
  0.6 70.2 %layer.1 = (bf16[16,8192]{1,0:T(8,128)(2,1)}, f32[4,512]{1,0:T(4,128)}, f32[2,256]{1,0:T(2,128)}, f32[2,256]{1,0:T(2,128)}) custom-call(bf16[16,8192]{1,0:T(8,128)(2,1)} %x_hbm.1, f32[4,512]{1,0:T(4,128)} %w_hbm.1, f32[2,256]{1,0:T(2,128)} %logit_hbm.1, f32[2,256]{1,0:T(2,128)} %g_hbm.1, bf16[256,256]{1,0:T(8,128)(2,1)} %do_hbm.1, f32[2,128,128]{2,1,0:T(8,128)} %first_hbm.1, ...), custom_call_target="tpu_custom_call" | custom-call | tf_op jit(solution)/shard_map/layer/pallas_call | solution.py:688
  70.9 1.7 %settle.1 = (bf16[16,8192]{1,0:T(8,128)(2,1)}, f32[4,512]{1,0:T(4,128)}, f32[2,256]{1,0:T(2,128)}, f32[2,256]{1,0:T(2,128)}) custom-call(bf16[16,8192]{1,0:T(8,128)(2,1)} %get-tuple-element.8.refs_0_, f32[4,512]{1,0:T(4,128)} %get-tuple-element.9.refs_1_, f32[2,256]{1,0:T(2,128)} %get-tuple-element.10.refs_2_, f32[2,256]{1,0:T(2,128)} %get-tuple-element.11.refs_3_), custom_call_target="tpu_custom_call" | custom-call | tf_op jit(solution)/shard_map/settle/pallas_call | solution.py:727

commit v5 on v4

--- a/solution.py
+++ b/solution.py
@@ -120,7 +120,7 @@
     out_hbm, total_hbm, glogit_hbm, gdecay_hbm,
     w_ref, logit_ref, g_ref, do_ref, start, end,
     x_in, edge, ext, dext, conv_ref, sig_ref, qk_ref,
-    ratio_ref, gram_ref, score_ref, solve_ref, base_ref, weight_ref, push_ref,
+    ratio_ref, gram_ref, score_ref, solve_ref, base_ref, weight_ref, push_ref, pull_ref,
     a_mine, bc_mine, a_sib, bc_sib, row_a, col_a, cut_out, cut_in, row_bc, tile_out, tile_in,
     state_ref, own_ref, tail_ref, spill_ref, inbox, last_ref,
     gw_ref, gw_sib, gw_row, gw_col, total_ref, glogit_ref, gdecay_ref,
@@ -176,7 +176,7 @@
             buffer.at[x], buffer.at[x], col_send.at[kind, d], col_recv.at[kind, x], in_col(x)
         ).wait_recv()
 
-    row_steps, col_steps = range(1, row_len), range(1, col_len)
+    row_steps, col_steps = far_first(row_len), far_first(col_len)
 
     loads = [
         pltpu.make_async_copy(source, target, load_sem.at[i])
@@ -320,6 +320,14 @@
         )
     swap_a = remote(a_mine, a_sib, swap_send.at[0], swap_recv.at[0], sibling)
     swap_a.start()
+    for h in range(heads):
+        pull_ref[h] = mm(split(solve_ref[h]), split(tail_keys(h) * k), 0, 0)
+    a = convolve(1)
+    q = a * (inv_norm(a) * DK**-0.5)
+    qk_ref[:, :DK] = q
+    qk = mm(split(q), ks, 1, 1)
+    for h in range(heads):
+        score_ref[h] = ratio_ref[h] * qk
     swap_a.wait_recv()
     mine, theirs = a_mine[k_at], a_sib[k_at]
     a1 = split(jnp.where(low, mine, theirs))
@@ -332,24 +340,16 @@
     for d in row_steps:
         row_a_copy(d).start()
 
-    a = convolve(1)
-    q = a * (inv_norm(a) * DK**-0.5)
-    qk_ref[:, :DK] = q
-    qk = mm(split(q), ks, 1, 1)
     for load in loads[3:]:
         load.wait()
     for h in range(heads):
-        score_ref[h] = ratio_ref[h] * qk
-        score = split(score_ref[h])
         do = (do_ref[:, h * DV : (h + 1) * DV],)
-        reach = jnp.exp(col(h)) * q - mm(score, split(weight_ref[h]))
+        reach = jnp.exp(col(h)) * q - mm(split(score_ref[h]), split(weight_ref[h]))
         bc_mine[h, 1] = mm(do, split(reach), 0, 0)
-        push_ref[h] = mm(score, do, 0, 0)
     values = convolve(2)
     for h in range(heads):
-        base = mm(split(solve_ref[h]), split(beta(h) * values[:, h * DV : (h + 1) * DV]))
-        base_ref[h] = base
-        bc_mine[h, 0] = mm(split(base), split(tail_keys(h) * k), 0, 0)
+        written = split(beta(h) * values[:, h * DV : (h + 1) * DV])
+        bc_mine[h, 0] = mm(written, split(pull_ref[h]), 0, 0)
     swap_bc = remote(bc_mine, bc_sib, swap_send.at[1], swap_recv.at[1], sibling)
     swap_bc.start()
     for d in row_steps:
@@ -385,34 +385,72 @@
     cut_in[y_at] = cut_out[y_at]
     start[...] = start[...].T
     end[...] = end[...].T
+    for h in range(heads):
+        solve = split(solve_ref[h])
+        do = (do_ref[:, h * DV : (h + 1) * DV],)
+        push_ref[h] = mm(solve, split(mm(split(score_ref[h]), do, 0, 0)), 0, 0)
+        base_ref[h] = mm(solve, split(beta(h) * values[:, h * DV : (h + 1) * DV]))
     for d in row_steps:
         from_row(1, d, cut_in)
-    gained = {1: cut_in[0, :share, :]}
-    owed = {row_len - 2: cut_in[row_len - 1, share:, :]}
-    for t in range(1, row_len):
-        u = row_len - 1 - t
-        gained[t + 1] = mm(split(gained[t]), steps[t]) + cut_in[t, :share, :]
-        owed[u - 1] = mm(split(owed[u]), steps[u], 1, 1) + cut_in[u, share:, :]
-    row_bc[x_at, :share, :] = gained[row_len]
-    row_bc[x_at, share:, :] = owed[-1]
+    gives = [cut_in[y, :share, :] for y in range(row_len)]
+    takes = [cut_in[y, share:, :] for y in range(row_len)]
+    row_give, row_take = gives[row_len - 1], takes[0]
+    for y in range(row_len - 1):
+        row_give = row_give + mm(split(gives[y]), ahead[y])
+        row_take = row_take + mm(split(takes[y + 1]), behind[y + 1], 1, 1)
+    row_bc[x_at, :share, :] = row_give
+    row_bc[x_at, share:, :] = row_take
 
     def row_bc_copy(d):
         return to_col(1, d, row_bc.at[x_at], row_bc.at[x_at])
 
     for d in col_steps:
         row_bc_copy(d).start()
+    gained = {1: gives[0]}
+    owed = {row_len - 2: takes[row_len - 1]}
+    for t in range(1, row_len - 1):
+        u = row_len - 1 - t
+        gained[t + 1] = mm(split(gained[t]), steps[t]) + gives[t]
+        owed[u - 1] = mm(split(owed[u]), steps[u], 1, 1) + takes[u]
     my_rows = pl.ds(pl.multiple_of(y_at * share, share), share)
     s, d_state = start[my_rows, :], end[my_rows, :]
     for d in col_steps:
         from_col(0, d, col_a)
     leaps = [split(col_a[x]) for x in range(col_len)]
+    between = {}
+    for t in range(-1, col_len):
+        for x in range(t + 2, col_len + 1):
+            reach = leaps[x - 1]
+            between[t, x] = reach if x == t + 2 else split(mm(between[t, x - 1], reach))
+
+    def pick(choices):
+        hi, lo = choices[0][1]
+        for x, part in choices[1:]:
+            hi = jnp.where(x_at == x, part[0], hi)
+            lo = jnp.where(x_at == x, part[1], lo)
+        return hi, lo
+
+    def carried(t, value):
+        far_rows = [(x, between[t, x]) for x in range(t + 2, col_len)]
+        near_term = jnp.where(x_at == t + 1, value, 0.0)
+        if not far_rows:
+            return near_term
+        return jnp.where(x_at > t + 1, mm(split(value), pick(far_rows)), near_term)
+
+    def carried_back(t, value):
+        far_rows = [(x, between[x, t]) for x in range(t - 1)]
+        near_term = jnp.where(x_at == t - 1, value, 0.0)
+        if not far_rows:
+            return near_term
+        return jnp.where(x_at < t - 1, mm(split(value), pick(far_rows), 1, 1), near_term)
+
+    s, d_state = carried(-1, s), carried_back(col_len, d_state)
     for d in col_steps:
         from_col(1, d, row_bc)
     for t in range(col_len - 1):
         u = col_len - 1 - t
-        s = jnp.where(t < x_at, mm(split(s), leaps[t]) + row_bc[t, :share, :], s)
-        back = mm(split(d_state), leaps[u], 1, 1) + row_bc[u, share:, :]
-        d_state = jnp.where(u > x_at, back, d_state)
+        s = s + carried(t, row_bc[t, :share, :])
+        d_state = d_state + carried_back(u, row_bc[u, share:, :])
     ss, ds = split(s), split(d_state)
     for y in range(row_len):
         tile_out[y, :share, :] = mm(ss, behind[y]) + gained[y] if y else s
@@ -501,27 +539,23 @@
         sts, dsts = split(state_ref[h, 0]), split(state_ref[h, 1])
         tail_k = tail_keys(h) * k
         update = base_ref[h] - mm(split(weight_ref[h]), sts, 1, 1)
-        d_update = push_ref[h] + mm(split(tail_k), dsts, 1, 1)
-        x = mm(split(solve_ref[h]), split(d_update), 0, 0)
+        x = push_ref[h] + mm(split(pull_ref[h]), dsts, 1, 1)
         span = slice(2 * DK + h * DV, 2 * DK + (h + 1) * DV)
         dext[EDGE : EDGE + rows, span] = (beta(h) * x) * silu_slope(span)
-        v = conv_ref[:, span] * sig_ref[:, span]
-        kept.append((sts, dsts, tail_k, split(update), split(x), jnp.sum(x * v, axis=1, keepdims=True)))
+        kept.append((sts, dsts, tail_k, split(update), x))
     unconvolve(0)
     dq = None
-    row_terms, col_terms = [], []
-    for h in range(heads):
-        sts, dsts, tail_k, us, xs, xv = kept[h]
+    sides = []
+    for h in range(heads):
+        sts, dsts, tail_k, us, x = kept[h]
+        xs = split(x)
         decays = jnp.exp(col(h))
-        total_decay = jnp.exp(col(h)[rows - 1 : rows, :])
         ratios = ratio_ref[h]
-        score = score_ref[h]
         do = (do_ref[:, h * DV : (h + 1) * DV],)
         d_score = mm(do, us, 1, 1)
         d_low = -mm(xs, us, 1, 1)
         y = -mm(xs, sts)
         d_tail = mm(us, dsts)
-        rgd = gram_ref[h] * d_low
         part_q = decays * mm(do, sts)
         part_k = tail_keys(h) * d_tail + (beta(h) * decays) * y
         z = ratios * d_score
@@ -530,22 +564,7 @@
             dq, dk, zs, dgs = part_q, part_k, z, d_gram
         else:
             dq, dk, zs, dgs = dq + part_q, dk + part_k, zs + z, dgs + d_gram
-        flow = jnp.where(lower, score * d_score, 0.0) + beta(h) * rgd
-        yk = decays * jnp.sum(y * k, axis=1, keepdims=True)
-        tk = jnp.sum(tail_k * d_tail, axis=1, keepdims=True)
-        d_beta = xv + yk + jnp.sum(rgd, axis=1, keepdims=True)
-        d_cum = (
-            jnp.sum(flow, axis=1, keepdims=True)
-            + jnp.sum(q * part_q, axis=1, keepdims=True)
-            + beta(h) * yk
-            - tk
-        )
-        ends = total_decay * jnp.sum(
-            state_ref[h, 0] * state_ref[h, 1], keepdims=True
-        ) + jnp.sum(tk, keepdims=True)
-        at_end = lax.broadcasted_iota(jnp.int32, (rows, 1), 0) == rows - 1
-        col_terms.append((d_cum + jnp.where(at_end, ends, 0.0), d_beta))
-        row_terms.append(jnp.sum(flow, axis=0, keepdims=True))
+        sides.append((d_score, d_low, y, d_tail, part_q))
     zs, dgs = split(zs), split(dgs)
     dq = dq + mm(zs, ks)
     dk = dk + mm(zs, qs, 0, 0) + mm(dgs, ks) + mm(dgs, ks, 0, 0)
@@ -597,6 +616,30 @@
 
     for d in row_steps:
         gw_row_copy(d).start()
+    row_terms, col_terms = [], []
+    for h in range(heads):
+        d_score, d_low, y, d_tail, part_q = sides[h]
+        span = slice(2 * DK + h * DV, 2 * DK + (h + 1) * DV)
+        tail_k, x = kept[h][2], kept[h][4]
+        xv = jnp.sum(x * (conv_ref[:, span] * sig_ref[:, span]), axis=1, keepdims=True)
+        total_decay = jnp.exp(col(h)[rows - 1 : rows, :])
+        rgd = gram_ref[h] * d_low
+        flow = jnp.where(lower, score_ref[h] * d_score, 0.0) + beta(h) * rgd
+        yk = jnp.exp(col(h)) * jnp.sum(y * k, axis=1, keepdims=True)
+        tk = jnp.sum(tail_k * d_tail, axis=1, keepdims=True)
+        d_beta = xv + yk + jnp.sum(rgd, axis=1, keepdims=True)
+        d_cum = (
+            jnp.sum(flow, axis=1, keepdims=True)
+            + jnp.sum(q * part_q, axis=1, keepdims=True)
+            + beta(h) * yk
+            - tk
+        )
+        ends = total_decay * jnp.sum(
+            state_ref[h, 0] * state_ref[h, 1], keepdims=True
+        ) + jnp.sum(tk, keepdims=True)
+        at_end = lax.broadcasted_iota(jnp.int32, (rows, 1), 0) == rows - 1
+        col_terms.append((d_cum + jnp.where(at_end, ends, 0.0), d_beta))
+        row_terms.append(jnp.sum(flow, axis=0, keepdims=True))
     lanes = lax.broadcasted_iota(jnp.int32, (rows, 8), 1)
     packed = jnp.zeros((rows, 8), f32)
     for h in range(heads):
@@ -701,7 +744,7 @@
             vm((rows, width), bf16), vm((EDGE, width), bf16),
             vm((EDGE + rows, width), f32), vm((2 * EDGE + rows, width), f32),
             vm((rows, width), f32), vm((rows, width), f32), vm((rows, 2 * DK), f32),
-            square, square, square, square, tall, tall, tall,
+            square, square, square, square, tall, tall, tall, tall,
             vm((heads, DK, DK), f32), vm((heads, 2, DV, DK), f32),
             vm((heads, DK, DK), f32), vm((heads, 2, DV, DK), f32),
             vm((row_len, DK, DK), f32), vm((col_len, DK, DK), f32),

time: 72.7 us -> 69.1 us (0.950)
  Pallas kernels: 71.9 us -> 68.3 us
    pallas_call x1, Pallas kernels: 70.2 us -> 66.6 us  [on_device(): pl.pallas_call(functools.partial(layer_kernel, n, nc, row_len), out_shape...]
where the time goes in v5:
time: 69.1 us; the launch traced here: 69 us
  Pallas kernels  68.3 us (99%)
    pallas_call x1, Pallas kernels, on_device(): pl.pallas_call(functools.partial(layer_kernel, n, nc, row_len), out_shape...  66.6 us
    pallas_call x1, Pallas kernels, on_device(): pl.pallas_call(settle_kernel, out_shape=tuple((shape_of(*part.shape, dtyp...  1.7 us

profile of v5, /device:TPU:1, one launch (start us, length us, event | category | flops | bytes accessed | tf_op | source)
XLA Modules:
  0.0 69.0 jit_solution(13087223582109822769)
XLA Ops:
  0.6 66.6 %layer.1 = (bf16[16,8192]{1,0:T(8,128)(2,1)}, f32[4,512]{1,0:T(4,128)}, f32[2,256]{1,0:T(2,128)}, f32[2,256]{1,0:T(2,128)}) custom-call(bf16[16,8192]{1,0:T(8,128)(2,1)} %x_hbm.1, f32[4,512]{1,0:T(4,128)} %w_hbm.1, f32[2,256]{1,0:T(2,128)} %logit_hbm.1, f32[2,256]{1,0:T(2,128)} %g_hbm.1, bf16[256,256]{1,0:T(8,128)(2,1)} %do_hbm.1, f32[2,128,128]{2,1,0:T(8,128)} %first_hbm.1, ...), custom_call_target="tpu_custom_call" | custom-call | tf_op jit(solution)/shard_map/layer/pallas_call | solution.py:731
  67.3 1.7 %settle.1 = (bf16[16,8192]{1,0:T(8,128)(2,1)}, f32[4,512]{1,0:T(4,128)}, f32[2,256]{1,0:T(2,128)}, f32[2,256]{1,0:T(2,128)}) custom-call(bf16[16,8192]{1,0:T(8,128)(2,1)} %get-tuple-element.8.refs_0_, f32[4,512]{1,0:T(4,128)} %get-tuple-element.9.refs_1_, f32[2,256]{1,0:T(2,128)} %get-tuple-element.10.refs_2_, f32[2,256]{1,0:T(2,128)} %get-tuple-element.11.refs_3_), custom_call_target="tpu_custom_call" | custom-call | tf_op jit(solution)/shard_map/settle/pallas_call | solution.py:770
